TPU v7x, 512 devices: a whole 4x4x16 slice. The times are simulated.
512 devices in a mesh: dp: 32 (over z, core), seq: 16 (over y, x).
Axes of the slice: x: 4, y: 4, z: 16, core: 2. Of those that a mesh axis runs over, the one named last changes fastest.
Arguments:
- q_pre: bfloat16 [32, 2048, 16, 128], P('dp', 'seq'), may hold values from -6 to 6
- k_pre: bfloat16 [32, 2048, 8, 128], P('dp', 'seq'), may hold values from -6 to 6
- values: bfloat16 [32, 2048, 8, 128], P('dp', 'seq'), may hold values from -6 to 6
- grad_out: bfloat16 [32, 2048, 16, 128], P('dp', 'seq'), may hold values from -6 to 6
- segment_ids: int32 [32, 2048], P('dp', 'seq'), may hold values from 0 to 7, never falling along the last dimension, each value on 1 to 1024 neighbouring positions
- q_gain: float32 [128], replicated, may hold values from 0.1 to 1.9
- k_gain: float32 [128], replicated, may hold values from 0.1 to 1.9
Outputs:
- grad_q: bfloat16 [32, 2048, 16, 128], P('dp', 'seq')
- grad_k: bfloat16 [32, 2048, 8, 128], P('dp', 'seq')
- grad_v: bfloat16 [32, 2048, 8, 128], P('dp', 'seq')
- grad_q_gain: float32 [128], replicated
- grad_k_gain: float32 [128], replicated
Inputs may be any that keep to these rules, and one draw needn't show every extreme that they name: `segment_ids`: along a span the ids never fall, and each id from 0 to 7 names one run of consecutive tokens.
All inputs are finite; a program needn't handle non-finite values.
Results may differ from a plain program's by a relative error of at most 0.017.
Values may be sent and summed in bfloat16 or wider, within the bound.
A program may use at most 64 MiB of HBM per device.

v0:
```python
import jax
import jax.numpy as jnp
from jax import lax
from jax.sharding import PartitionSpec as P

PRESCALE = 168
DOCS = 8


norm_epsilon = 1e-06
rope_base = 1000000.0
rope_factor = 8.0


def document_positions(segments, docs):
    labels = jnp.arange(docs, dtype=jnp.int32)
    member = (segments[:, None] == labels[None, :]).astype(jnp.int32)
    counts = jnp.sum(member, axis=0)
    starts = jnp.cumsum(counts) - counts
    first = jnp.sum(member * starts[None, :], axis=1)
    return (jnp.arange(segments.shape[0], dtype=jnp.int32) - first, first)


def embed(rows, gain, positions):
    width = rows.shape[-1]
    half = width // 2
    scale = lax.rsqrt(jnp.mean(rows * rows, axis=-1, keepdims=True) + norm_epsilon)
    normed = rows * scale * gain
    freqs = rope_base ** (-(jnp.arange(half, dtype=jnp.float32) * 2.0 / width))
    angles = (positions.astype(jnp.float32) / rope_factor)[:, None] * freqs[None, :]
    cosine = jnp.cos(angles)[:, None, :]
    sine = jnp.sin(angles)[:, None, :]
    first_half = normed[..., :half]
    second_half = normed[..., half:]
    return jnp.concatenate(
        [first_half * cosine - second_half * sine, second_half * cosine + first_half * sine],
        axis=-1,
    )


def attend_blocks(queries, keys, vals, upstream, segments):
    total = queries.shape[0]
    group = queries.shape[1]
    width = queries.shape[2]
    block = min(512, total)
    count = total // block
    rows = block * group
    score_scale = float(PRESCALE) ** (-0.5)
    contract_last = (((1,), (1,)), ((), ()))
    contract_first = (((0,), (0,)), ((), ()))

    def query_block(query_index, carry):
        query_grads, key_grads, value_grads = carry
        start = query_index * block
        query_rows = lax.dynamic_slice_in_dim(queries, start, block, 0).reshape(rows, width)
        upstream_rows = lax.dynamic_slice_in_dim(upstream, start, block, 0).reshape(rows, width)
        query_segs = jnp.repeat(lax.dynamic_slice_in_dim(segments, start, block, 0), group)
        query_places = jnp.repeat(start + jnp.arange(block, dtype=jnp.int32), group)
        lower = 0

        def key_scores(key_index):
            key_start = key_index * block
            key_rows = lax.dynamic_slice_in_dim(keys, key_start, block, 0)
            value_rows = lax.dynamic_slice_in_dim(vals, key_start, block, 0)
            key_segs = lax.dynamic_slice_in_dim(segments, key_start, block, 0)
            key_places = key_start + jnp.arange(block, dtype=jnp.int32)
            scores = score_scale * lax.dot_general(
                query_rows, key_rows, contract_last, preferred_element_type=jnp.float32
            )
            visible = (query_segs[:, None] == key_segs[None, :]) & (
                query_places[:, None] >= key_places[None, :]
            )
            return (scores, visible, key_rows, value_rows, key_start)

        def forward_step(key_index, state):
            totals, numer = state
            scores, visible, key_rows, value_rows, key_start = key_scores(key_index)
            raw = jnp.where(visible, jnp.exp(scores), 0.0)
            numer = numer + jnp.dot(
                raw.astype(jnp.bfloat16), value_rows, preferred_element_type=jnp.float32
            )
            return (totals + jnp.sum(raw, axis=1), numer)

        totals, numer = lax.fori_loop(
            lower,
            query_index + 1,
            forward_step,
            (jnp.zeros((rows,), jnp.float32), jnp.zeros((rows, width), jnp.float32)),
        )
        outputs = numer / totals[:, None]
        delta = jnp.sum(upstream_rows.astype(jnp.float32) * outputs, axis=1)
        logsum = jnp.log(totals)

        def backward_step(key_index, state):
            query_part, key_acc, value_acc = state
            scores, visible, key_rows, value_rows, key_start = key_scores(key_index)
            probs = jnp.where(visible, jnp.exp(scores - logsum[:, None]), 0.0).astype(jnp.bfloat16)
            prob_grads = lax.dot_general(
                upstream_rows, value_rows, contract_last, preferred_element_type=jnp.float32
            )
            score_grads = (
                probs.astype(jnp.float32) * (prob_grads - delta[:, None]) * score_scale
            ).astype(jnp.bfloat16)
            query_part = query_part + jnp.dot(
                score_grads, key_rows, preferred_element_type=jnp.float32
            )
            key_part = lax.dot_general(
                score_grads, query_rows, contract_first, preferred_element_type=jnp.float32
            )
            value_part = lax.dot_general(
                probs, upstream_rows, contract_first, preferred_element_type=jnp.float32
            )
            key_acc = lax.dynamic_update_slice_in_dim(
                key_acc,
                lax.dynamic_slice_in_dim(key_acc, key_start, block, 0) + key_part,
                key_start,
                0,
            )
            value_acc = lax.dynamic_update_slice_in_dim(
                value_acc,
                lax.dynamic_slice_in_dim(value_acc, key_start, block, 0) + value_part,
                key_start,
                0,
            )
            return (query_part, key_acc, value_acc)

        query_part, key_grads, value_grads = lax.fori_loop(
            lower,
            query_index + 1,
            backward_step,
            (jnp.zeros((rows, width), jnp.float32), key_grads, value_grads),
        )
        query_grads = lax.dynamic_update_slice_in_dim(query_grads, query_part, start * group, 0)
        return (query_grads, key_grads, value_grads)

    initial = (
        jnp.zeros((total * group, width), jnp.float32),
        jnp.zeros((total, width), jnp.float32),
        jnp.zeros((total, width), jnp.float32),
    )
    query_grads, key_grads, value_grads = lax.fori_loop(0, count, query_block, initial)
    return (query_grads.reshape(total, group, width), key_grads, value_grads)


def body(q_pre, k_pre, values, grad_out, segment_ids, q_gain, k_gain):
    segments = lax.all_gather(segment_ids, "seq", axis=1, tiled=True)[0]
    positions, first = document_positions(segments, DOCS)
    local = q_pre.shape[1]
    heads = q_pre.shape[2]
    kv_heads = k_pre.shape[2]
    width = q_pre.shape[3]
    group = heads // kv_heads

    def embed_rows(rows, gain):
        return embed(rows, gain, positions)

    key_copies = jnp.repeat(k_pre[0], group, axis=1)
    value_copies = jnp.repeat(values[0], group, axis=1)
    query_here, upstream_here, key_here, value_here = (
        lax.all_to_all(q_pre[0], "seq", split_axis=1, concat_axis=0, tiled=True),
        lax.all_to_all(grad_out[0], "seq", split_axis=1, concat_axis=0, tiled=True),
        lax.all_to_all(key_copies, "seq", split_axis=1, concat_axis=0, tiled=True),
        lax.all_to_all(value_copies, "seq", split_axis=1, concat_axis=0, tiled=True),
    )
    query_rot, query_back = jax.vjp(embed_rows, query_here.astype(jnp.float32), q_gain)
    key_rot, key_back = jax.vjp(embed_rows, key_here.astype(jnp.float32), k_gain)
    query_hat = query_rot.astype(jnp.bfloat16)
    key_hat = key_rot.astype(jnp.bfloat16)
    query_list, key_list, value_list = ([], [], [])
    query_part, key_part, value_part = attend_blocks(
        query_hat, key_hat[:, 0], value_here[:, 0], upstream_here, segments
    )
    query_list.append(query_part)
    key_list.append(key_part)
    value_list.append(value_part)
    query_input, query_gain_part = query_back(query_list[0])
    key_input, key_gain_part = key_back(jnp.stack(key_list, axis=1))
    value_input = jnp.stack(value_list, axis=1)
    query_return, key_return, value_return = (
        lax.all_to_all(
            query_input.astype(jnp.bfloat16), "seq", split_axis=0, concat_axis=1, tiled=True
        ).astype(query_input.dtype),
        lax.all_to_all(
            key_input.astype(jnp.bfloat16), "seq", split_axis=0, concat_axis=1, tiled=True
        ).astype(key_input.dtype),
        lax.all_to_all(
            value_input.astype(jnp.bfloat16), "seq", split_axis=0, concat_axis=1, tiled=True
        ).astype(value_input.dtype),
    )
    grad_q = query_return.astype(jnp.bfloat16)
    grad_k = jnp.sum(key_return.reshape(local, kv_heads, group, width), axis=2).astype(jnp.bfloat16)
    grad_v = jnp.sum(value_return.reshape(local, kv_heads, group, width), axis=2).astype(
        jnp.bfloat16
    )
    gain_totals = lax.psum((query_gain_part, key_gain_part), ("dp", "seq"))
    return (grad_q[None], grad_k[None], grad_v[None], gain_totals[0], gain_totals[1])


def solution(mesh):
    return jax.shard_map(
        body,
        mesh=mesh,
        in_specs=(
            P("dp", "seq", None, None),
            P("dp", "seq", None, None),
            P("dp", "seq", None, None),
            P("dp", "seq", None, None),
            P("dp", "seq"),
            P(),
            P(),
        ),
        out_specs=(
            P("dp", "seq", None, None),
            P("dp", "seq", None, None),
            P("dp", "seq", None, None),
            P(),
            P(),
        ),
        check_vma=False,
    )
```

profile of v0, /device:TPU:1, one launch (start us, length us, event | category | flops | bytes accessed | tf_op | source)
XLA Modules:
  0.0 308.5 jit_solution(509402824562934716)
XLA Ops:
  2.6 7.7 %all-to-all-start = ((bf16[128,16,128]{2,0,1:T(8,128)(2,1)}), bf16[128,16,128]{2,0,1:T(8,128)(2,1)S(1)}, u32[]{:S(2)}, u32[]{:S(2)}) async-start(bf16[128,16,128]{2,0,1:T(8,128)(2,1)} %bitcast.130), calls=%async_computation | async-start | bytes 1048576 | tf_op jit(solution)/shard_map/all_to_all | solution.py:160
  10.4 17.6 %all_gather.3 = s32[1,2048]{1,0:T(1,128)S(1)} all-gather(s32[1,128]{1,0:T(1,128)S(1)} %copy-done.13), channel_id=1, replica_groups=mesh['dp'=32,'seq'=16] {'seq'}, dimensions={1}, use_global_device_ids=true | all-gather | bytes 8704 | tf_op jit(solution)/shard_map/all_gather | solution.py:146
  31.3 4.0 %all-to-all-start.1 = ((bf16[128,16,128]{0,2,1:T(8,128)(2,1)}), bf16[128,16,128]{0,2,1:T(8,128)(2,1)S(1)}, u32[]{:S(2)}, u32[]{:S(2)}) async-start(bf16[128,16,128]{0,2,1:T(8,128)(2,1)} %bitcast.12), calls=%async_computation.1 | async-start | bytes 1048576 | tf_op jit(solution)/shard_map/all_to_all | solution.py:162
  37.4 6.9 %all-to-all-done.1 = bf16[128,16,128]{0,2,1:T(8,128)(2,1)S(1)} async-done(((bf16[128,16,128]{0,2,1:T(8,128)(2,1)}), bf16[128,16,128]{0,2,1:T(8,128)(2,1)S(1)}, u32[]{:S(2)}, u32[]{:S(2)}) %all-to-all-start.1) | async-done | bytes 524320 | tf_op jit(solution)/shard_map/all_to_all | solution.py:162
  45.3 3.6 %all-to-all-start.2 = ((bf16[128,16,128]{2,0,1:T(8,128)(2,1)}), bf16[128,16,128]{2,0,1:T(8,128)(2,1)S(1)}, u32[]{:S(2)}, u32[]{:S(2)}) async-start(bf16[128,16,128]{2,0,1:T(8,128)(2,1)} %bitcast.20), calls=%async_computation.2 | async-start | bytes 1048576 | tf_op jit(solution)/shard_map/all_to_all | solution.py:163
  50.8 7.0 %all-to-all-done.2 = bf16[128,16,128]{2,0,1:T(8,128)(2,1)S(1)} async-done(((bf16[128,16,128]{2,0,1:T(8,128)(2,1)}), bf16[128,16,128]{2,0,1:T(8,128)(2,1)S(1)}, u32[]{:S(2)}, u32[]{:S(2)}) %all-to-all-start.2) | async-done | bytes 524320 | tf_op jit(solution)/shard_map/all_to_all | solution.py:163
  57.8 4.2 %all-to-all-start.3 = ((bf16[128,16,128]{2,0,1:T(8,128)(2,1)}), bf16[128,16,128]{2,0,1:T(8,128)(2,1)}, u32[]{:S(2)}, u32[]{:S(2)}) async-start(bf16[128,16,128]{2,0,1:T(8,128)(2,1)} %bitcast.129), calls=%async_computation.3 | async-start | bytes 1048576 | tf_op jit(solution)/shard_map/all_to_all | solution.py:161
  62.1 3.1 fusion.63
  66.2 4.8 %all-to-all-done.3 = bf16[128,16,128]{2,0,1:T(8,128)(2,1)} async-done(((bf16[128,16,128]{2,0,1:T(8,128)(2,1)}), bf16[128,16,128]{2,0,1:T(8,128)(2,1)}, u32[]{:S(2)}, u32[]{:S(2)}) %all-to-all-start.3) | async-done | bytes 524320 | tf_op jit(solution)/shard_map/all_to_all | solution.py:161
  72.3 69.1 %while.79 = (s32[]{:T(128)}, f32[2048,128]{0,1:T(8,128)}, f32[2048,128]{1,0:T(8,128)S(1)}, f32[2048,128]{1,0:T(8,128)S(1)}, bf16[2048,1,128]{0,2,1:T(8,128)(2,1)...) while((s32[]{:T(128)}, f32[2048,128]{0,1:T(8,128)}, ...), condition=%wide.region_12.13_spmd, body=%wide.region_5.12_spmd.sunk | while | flops 475268608 | bytes 14478353 | solution.py:141
  76.3 3.7 %while.81 = (s32[]{:T(128)}, f32[512,128]{1,0:T(8,128)S(1)}, f32[2048,128]{1,0:T(8,128)S(1)}, f32[2048,128]{1,0:T(8,128)S(1)}, s32[]{:T(128)}, /*index=5*/s32[51...) while((s32[]{:T(128)}, f32[512,128]{1,0:T(8,128)S(1)}, ...), condition=%wide.region_11.11_spmd.clone, body=%wide.region_10.10_spmd.clone.sunk | while | flops 338887680 | bytes 5656819 | solution.py:127
  82.1 3.7 %while.80 = (s32[]{:T(128)}, f32[512]{0:T(512)S(1)}, f32[512,128]{1,0:T(8,128)S(1)}, s32[]{:T(128)}, s32[512]{0:T(512)S(1)}, /*index=5*/s32[2048]{0:T(1024)S(1)}...) while((s32[]{:T(128)}, f32[512]{0:T(512)S(1)}, ...), condition=%wide.region_8.8_spmd.clone, body=%wide.region_6.7_spmd.clone.sunk | while | flops 136119296 | bytes 1990855 | solution.py:84
  87.0 7.4 %while.81 = (s32[]{:T(128)}, f32[512,128]{1,0:T(8,128)S(1)}, f32[2048,128]{1,0:T(8,128)S(1)}, f32[2048,128]{1,0:T(8,128)S(1)}, s32[]{:T(128)}, /*index=5*/s32[51...) while((s32[]{:T(128)}, f32[512,128]{1,0:T(8,128)S(1)}, ...), condition=%wide.region_11.11_spmd.clone, body=%wide.region_10.10_spmd.clone.sunk | while | flops 338887680 | bytes 5656819 | solution.py:127
  96.6 5.6 %while.80 = (s32[]{:T(128)}, f32[512]{0:T(512)S(1)}, f32[512,128]{1,0:T(8,128)S(1)}, s32[]{:T(128)}, s32[512]{0:T(512)S(1)}, /*index=5*/s32[2048]{0:T(1024)S(1)}...) while((s32[]{:T(128)}, f32[512]{0:T(512)S(1)}, ...), condition=%wide.region_8.8_spmd.clone, body=%wide.region_6.7_spmd.clone.sunk | while | flops 136119296 | bytes 1990855 | solution.py:84
  103.4 11.1 %while.81 = (s32[]{:T(128)}, f32[512,128]{1,0:T(8,128)S(1)}, f32[2048,128]{1,0:T(8,128)S(1)}, f32[2048,128]{1,0:T(8,128)S(1)}, s32[]{:T(128)}, /*index=5*/s32[51...) while((s32[]{:T(128)}, f32[512,128]{1,0:T(8,128)S(1)}, ...), condition=%wide.region_11.11_spmd.clone, body=%wide.region_10.10_spmd.clone.sunk | while | flops 338887680 | bytes 5656819 | solution.py:127
  116.6 7.5 %while.80 = (s32[]{:T(128)}, f32[512]{0:T(512)S(1)}, f32[512,128]{1,0:T(8,128)S(1)}, s32[]{:T(128)}, s32[512]{0:T(512)S(1)}, /*index=5*/s32[2048]{0:T(1024)S(1)}...) while((s32[]{:T(128)}, f32[512]{0:T(512)S(1)}, ...), condition=%wide.region_8.8_spmd.clone, body=%wide.region_6.7_spmd.clone.sunk | while | flops 136119296 | bytes 1990855 | solution.py:84
  125.3 14.8 %while.81 = (s32[]{:T(128)}, f32[512,128]{1,0:T(8,128)S(1)}, f32[2048,128]{1,0:T(8,128)S(1)}, f32[2048,128]{1,0:T(8,128)S(1)}, s32[]{:T(128)}, /*index=5*/s32[51...) while((s32[]{:T(128)}, f32[512,128]{1,0:T(8,128)S(1)}, ...), condition=%wide.region_11.11_spmd.clone, body=%wide.region_10.10_spmd.clone.sunk | while | flops 338887680 | bytes 5656819 | solution.py:127
  142.7 4.1 %fusion.60 = (f32[2048,1,64]{0,2,1:T(8,128)S(1)}, f32[2048,1,64]{0,2,1:T(8,128)S(1)}, f32[2048,1,64]{0,2,1:T(8,128)S(1)}, f32[2048,1,64]{0,2,1:T(8,128)S(1)}) fusion(f32[2048,1,128]{0,2,1:T(8,128)} %bitcast.158, f32[64]{0:T(128)S(1)} %negate_power_fusion, f32[2048]{0:T(1024)S(1)} %convert_multiply_fusion.1, f32[2048,1,128]{0,2,1:T(8,128)} %bitcast.157), kind=kLoop, calls=%fused_computation.89 | loop fusion | flops 1966080 | bytes 4202752 | tf_op jit(solution)/shard_map/transpose(jvp())/add_any | solution.py:36
  151.6 3.6 %all-to-all-start.4 = ((bf16[16,2,8192]{2,1,0:T(2,128)(2,1)}), bf16[16,2,8192]{2,1,0:T(2,128)(2,1)S(1)}, u32[]{:S(2)}, u32[]{:S(2)}) async-start(bf16[16,2,8192]{2,1,0:T(2,128)(2,1)} %reshape.576), calls=%async_computation.4 | async-start | bytes 1048576 | tf_op jit(solution)/shard_map/all_to_all | solution.py:180
  157.4 6.8 %all-to-all-done.4 = bf16[16,2,8192]{2,1,0:T(2,128)(2,1)S(1)} async-done(((bf16[16,2,8192]{2,1,0:T(2,128)(2,1)}), bf16[16,2,8192]{2,1,0:T(2,128)(2,1)S(1)}, u32[]{:S(2)}, u32[]{:S(2)}) %all-to-all-start.4) | async-done | bytes 524320 | tf_op jit(solution)/shard_map/all_to_all | solution.py:180
  164.1 3.6 %all-to-all-start.5 = ((bf16[16,2,8192]{2,1,0:T(2,128)(2,1)}), bf16[16,2,8192]{2,1,0:T(2,128)(2,1)S(1)}, u32[]{:S(2)}, u32[]{:S(2)}) async-start(bf16[16,2,8192]{2,1,0:T(2,128)(2,1)} %reshape.578), calls=%async_computation.5 | async-start | bytes 1048576 | tf_op jit(solution)/shard_map/all_to_all | solution.py:183
  169.7 9.0 %all-to-all-done.5 = bf16[16,2,8192]{2,1,0:T(2,128)(2,1)S(1)} async-done(((bf16[16,2,8192]{2,1,0:T(2,128)(2,1)}), bf16[16,2,8192]{2,1,0:T(2,128)(2,1)S(1)}, u32[]{:S(2)}, u32[]{:S(2)}) %all-to-all-start.5) | async-done | bytes 524320 | tf_op jit(solution)/shard_map/all_to_all | solution.py:183
  178.7 3.6 %all-to-all-start.6 = ((bf16[16,2,8192]{2,1,0:T(2,128)(2,1)}), bf16[16,2,8192]{2,1,0:T(2,128)(2,1)S(1)}, u32[]{:S(2)}, u32[]{:S(2)}) async-start(bf16[16,2,8192]{2,1,0:T(2,128)(2,1)} %reshape.580), calls=%async_computation.6 | async-start | bytes 1048576 | tf_op jit(solution)/shard_map/all_to_all | solution.py:186
  182.3 121.2 %all-reduce.4 = (f32[128]{0:T(128)}, f32[128]{0:T(128)}) all-reduce(f32[128]{0:T(128)S(1)} %get-tuple-element.430, f32[128]{0:T(128)S(1)} %get-tuple-element.428), channel_id=1, replica_groups=mesh['dp'=32,'seq'=16] {'dp','seq'}, use_global_device_ids=true, to_apply=%region_18.19 | all-reduce | flops 256 | bytes 2048 | tf_op jit(solution)/shard_map/psum | solution.py:195
  (256 shorter events, 97.5 us)
Async XLA Ops:
  2.6 7.7 %copy-start.13 = (s32[1,128]{1,0:T(1,128)S(1)}, s32[1,128]{1,0:T(1,128)}, u32[]{:S(2)}) copy-start(s32[1,128]{1,0:T(1,128)} %param.17) | copy-start | bytes 1540
  2.6 25.7 %copy-start.9 = (bf16[1,128,8,128]{3,2,1,0:T(8,128)(2,1)S(1)}, bf16[1,128,8,128]{3,2,1,0:T(8,128)(2,1)}, u32[]{:S(2)}) copy-start(bf16[1,128,8,128]{3,2,1,0:T(8,128)(2,1)} %param.14) | copy-start | bytes 786436
  2.6 27.8 %all-to-all-start = ((bf16[128,16,128]{2,0,1:T(8,128)(2,1)}), bf16[128,16,128]{2,0,1:T(8,128)(2,1)S(1)}, u32[]{:S(2)}, u32[]{:S(2)}) async-start(bf16[128,16,128]{2,0,1:T(8,128)(2,1)} %bitcast.130), calls=%async_computation | async-start | bytes 1048576 | tf_op jit(solution)/shard_map/all_to_all | solution.py:160
  10.3 18.2 %copy-start.10 = (bf16[1,128,8,128]{3,2,1,0:T(8,128)(2,1)S(1)}, bf16[1,128,8,128]{3,2,1,0:T(8,128)(2,1)}, u32[]{:S(2)}) copy-start(bf16[1,128,8,128]{3,2,1,0:T(8,128)(2,1)} %param.15) | copy-start | bytes 786436
  28.3 1.0 copy-start.8
  31.3 13.0 %all-to-all-start.1 = ((bf16[128,16,128]{0,2,1:T(8,128)(2,1)}), bf16[128,16,128]{0,2,1:T(8,128)(2,1)S(1)}, u32[]{:S(2)}, u32[]{:S(2)}) async-start(bf16[128,16,128]{0,2,1:T(8,128)(2,1)} %bitcast.12), calls=%async_computation.1 | async-start | bytes 1048576 | tf_op jit(solution)/shard_map/all_to_all | solution.py:162
  36.5 1.0 copy-start
  44.3 4.7 %copy-start.2 = (bf16[128,16,128]{0,2,1:T(8,128)(2,1)}, bf16[128,16,128]{0,2,1:T(8,128)(2,1)S(1)}, u32[]{:S(2)}) copy-start(bf16[128,16,128]{0,2,1:T(8,128)(2,1)S(1)} %all-to-all-done.1) | copy-start | bytes 1572868
  45.3 12.5 %all-to-all-start.2 = ((bf16[128,16,128]{2,0,1:T(8,128)(2,1)}), bf16[128,16,128]{2,0,1:T(8,128)(2,1)S(1)}, u32[]{:S(2)}, u32[]{:S(2)}) async-start(bf16[128,16,128]{2,0,1:T(8,128)(2,1)} %bitcast.20), calls=%async_computation.2 | async-start | bytes 1048576 | tf_op jit(solution)/shard_map/all_to_all | solution.py:163
  50.8 11.2 %copy-start.4 = (f32[2048,1,128]{0,2,1:T(8,128)S(1)}, f32[2048,1,128]{0,2,1:T(8,128)}, u32[]{:S(2)}) copy-start(f32[2048,1,128]{0,2,1:T(8,128)} %fusion.33) | copy-start | bytes 3145732
  57.8 13.2 %all-to-all-start.3 = ((bf16[128,16,128]{2,0,1:T(8,128)(2,1)}), bf16[128,16,128]{2,0,1:T(8,128)(2,1)}, u32[]{:S(2)}, u32[]{:S(2)}) async-start(bf16[128,16,128]{2,0,1:T(8,128)(2,1)} %bitcast.129), calls=%async_computation.3 | async-start | bytes 1048576 | tf_op jit(solution)/shard_map/all_to_all | solution.py:161
  65.2 1.0 copy-start.7
  72.4 0.8 copy-start.5
  80.1 1.1 copy-start.6
  94.6 1.1 copy-start.6
  95.7 0.8 copy-start.5
  114.6 1.1 copy-start.6
  115.8 0.8 copy-start.5
  140.3 1.1 copy-start.6
  142.7 4.1 %copy-start.3 = (bf16[128,16,128]{0,2,1:T(8,128)(2,1)S(1)}, bf16[128,16,128]{0,2,1:T(8,128)(2,1)}, u32[]{:S(2)}) copy-start(bf16[128,16,128]{0,2,1:T(8,128)(2,1)} %copy-done.2) | copy-start | bytes 1572868
  146.8 1.2 copy-start.1
  151.6 12.5 %all-to-all-start.4 = ((bf16[16,2,8192]{2,1,0:T(2,128)(2,1)}), bf16[16,2,8192]{2,1,0:T(2,128)(2,1)S(1)}, u32[]{:S(2)}, u32[]{:S(2)}) async-start(bf16[16,2,8192]{2,1,0:T(2,128)(2,1)} %reshape.576), calls=%async_computation.4 | async-start | bytes 1048576 | tf_op jit(solution)/shard_map/all_to_all | solution.py:180
  164.1 14.6 %all-to-all-start.5 = ((bf16[16,2,8192]{2,1,0:T(2,128)(2,1)}), bf16[16,2,8192]{2,1,0:T(2,128)(2,1)S(1)}, u32[]{:S(2)}, u32[]{:S(2)}) async-start(bf16[16,2,8192]{2,1,0:T(2,128)(2,1)} %reshape.578), calls=%async_computation.5 | async-start | bytes 1048576 | tf_op jit(solution)/shard_map/all_to_all | solution.py:183
  178.7 128.1 %all-to-all-start.6 = ((bf16[16,2,8192]{2,1,0:T(2,128)(2,1)}), bf16[16,2,8192]{2,1,0:T(2,128)(2,1)S(1)}, u32[]{:S(2)}, u32[]{:S(2)}) async-start(bf16[16,2,8192]{2,1,0:T(2,128)(2,1)} %reshape.580), calls=%async_computation.6 | async-start | bytes 1048576 | tf_op jit(solution)/shard_map/all_to_all | solution.py:186
  (3 other events, 2.1 us)
where the time goes:
time: 310 us; the launch traced here: 308 us
  blocking collectives  139 us (45%)
  matrix products  53.1 us (17%)
  waiting for transfers between devices  34.4 us (11%)
  local copies, waits for them, and re-layouts  30.6 us (10%)
  starting transfers between devices  30.2 us (10%)
  other arithmetic  19 us (6%)
    psum x1, blocking collectives, body(): gain_totals = lax.psum((query_gain_part, key_gain_part), ('dp', 'seq'))  121 us
    dot_general x20, matrix products, key_scores(): lax.dot_general(query_rows, key_rows, contract_last, preferred_element_ty...  27.3 us
    all_gather x1, blocking collectives, body(): segments = lax.all_gather(segment_ids, 'seq', axis=1, tiled=True)[0]  17.6 us
    unnamed x40, local copies, waits for them, and re-layouts  14.1 us
    dot_general x10, matrix products, backward_step(): jnp.dot(score_grads, key_rows, preferred_element_type=jnp.float32)  12.8 us
    all_to_all x1, waiting for transfers between devices, body(): lax.all_to_all(key_input.astype(jnp.bfloat16), 'seq', split_axis=0, conca...  8.96 us
    all_to_all x1, starting transfers between devices, body(): lax.all_to_all(q_pre[0], 'seq', split_axis=1, concat_axis=0, tiled=True)  7.72 us
    all_to_all x1, waiting for transfers between devices, body(): lax.all_to_all(value_copies, 'seq', split_axis=1, concat_axis=0, tiled=True)  6.98 us
  transfers between devices with their start and end apart: 7, of which 5 were waited for; matrix products, arithmetic and copies ran while one was open for 5% of the time, Pallas kernels for 0%

commit v1 on v0

v1 whole, which is shorter than its diff:
```python
import functools

import jax
import jax.numpy as jnp
import numpy as np
from jax import lax
from jax.experimental import pallas as pl
from jax.experimental.pallas import tpu as pltpu
from jax.sharding import PartitionSpec as P

PRESCALE = 168
HD = 128
SEQ = 16
TOK = 128
TOTAL = SEQ * TOK
BLK = 256
NBLK = TOTAL // BLK
BAND = 5
EPS = 1e-6
ROPE_BASE = 1000000.0
ROPE_FACTOR = 8.0
SCALE = float(PRESCALE) ** (-0.5)
QMUL = SCALE * float(np.log2(np.e))
LN2 = float(np.log(2.0))
MESH = pl.DeviceIdType.MESH
F32 = jnp.float32
BF16 = jnp.bfloat16
ANY = pl.BlockSpec(memory_space=pl.ANY)
VM = pl.BlockSpec(memory_space=pltpu.VMEM)


def rope_tables():
    half = HD // 2
    freqs = ROPE_BASE ** (-(np.arange(half, dtype=np.float64) * 2.0 / HD))
    freqs = np.concatenate([freqs, freqs])
    near = np.arange(TOK, dtype=np.float64)[:, None] / ROPE_FACTOR * freqs[None, :]
    far = np.arange(SEQ, dtype=np.float64)[:, None] * TOK / ROPE_FACTOR * freqs[None, :]
    return (
        np.stack([np.cos(near), np.sin(near)]).astype(np.float32),
        np.stack([np.cos(far), np.sin(far)], axis=1).astype(np.float32),
    )


def block_rope(near_ref, far_ref, block):
    far = far_ref[block]
    cb, sb = far[0:1, :], far[1:2, :]
    cosine = near_ref[0] * cb - near_ref[1] * sb
    sine = near_ref[1] * cb + near_ref[0] * sb
    lane = lax.broadcasted_iota(jnp.int32, (TOK, HD), 1)
    return cosine, jnp.where(lane < HD // 2, -sine, sine)


def turn(rows, cosine, sine):
    return rows * cosine + pltpu.roll(rows, HD // 2, 1) * sine


def turn_back(rows, cosine, sine):
    return rows * cosine - pltpu.roll(rows, HD // 2, 1) * sine


def place():
    dp = lax.axis_index("dp")
    s = lax.axis_index("seq")
    z = lax.div(dp, 2)
    return dp, s, z, lax.rem(dp, 2)


def greet(z, dp, s, core):
    barrier = pltpu.get_barrier_semaphore()

    def one(i, carry):
        peer_core, peer_seq = lax.div(i, SEQ), lax.rem(i, SEQ)

        @pl.when((peer_core != core) | (peer_seq != s))
        def _():
            pl.semaphore_signal(
                barrier, inc=1, device_id=(2 * z + peer_core, peer_seq), device_id_type=MESH
            )

        return carry

    lax.fori_loop(0, 2 * SEQ, one, 0)
    return barrier


def gather_kernel(
    q_hbm, k_hbm, v_hbm, g_hbm, seg_ref, qg_ref, kg_ref, near_ref, far_ref,
    q_out, g_out, kv_out, seg_out,
    q_raw, k_raw, v_raw, g_raw, q_wide, k_wide, v_wide, g_wide, q_buf, g_buf, kv_buf,
    load_sem, send_sem, recv_sem, pass_send, pass_recv,
):
    dp, s, z, core = place()
    loads = [
        pltpu.make_async_copy(src, dst, load_sem.at[i])
        for i, (src, dst) in enumerate(
            ((g_hbm, g_raw), (v_hbm, v_raw), (k_hbm, k_raw), (q_hbm, q_raw))
        )
    ]
    for copy in loads:
        copy.start()
    barrier = greet(z, dp, s, core)
    pl.semaphore_wait(barrier, 2 * SEQ - 1)

    def copies(kind, src, dst, j, r):
        peer_dp, peer_seq = 2 * z + r, 2 * j + core
        me = (peer_dp == dp) & (peer_seq == s)
        remote = pltpu.make_async_remote_copy(
            src_ref=src, dst_ref=dst, send_sem=send_sem.at[kind, 2 * j + r],
            recv_sem=recv_sem.at[kind, s], device_id=(peer_dp, peer_seq), device_id_type=MESH,
        )
        local = pltpu.make_async_copy(src, dst, recv_sem.at[kind, s])
        return me, remote, local

    def send(kind, src, dst, j, r):
        me, remote, local = copies(kind, src, dst, j, r)

        @pl.when(me)
        def _():
            local.start()

        @pl.when(jnp.logical_not(me))
        def _():
            remote.start()

    def sent(kind, src, dst, j, r):
        me, remote, local = copies(kind, src, dst, j, r)

        @pl.when(jnp.logical_not(me))
        def _():
            remote.wait_send()

    def turns(t):
        return lax.rem(lax.div(s, 2) + t, SEQ // 2)

    def parts(j, r):
        h = 2 * j + r
        return (
            (0, g_buf.at[h], g_out.at[s]),
            (1, kv_buf.at[r, j], kv_out.at[r, s]),
            (2, q_buf.at[h], q_out.at[s]),
            (3, seg_ref, seg_out.at[s]),
        )

    loads[0].wait()
    g_wide[...] = g_raw[...].astype(F32).reshape(TOK * 16, HD)

    def send_g(t, carry):
        j = turns(t)
        for r in range(2):
            h = 2 * j + r
            g_buf[h] = g_wide[pl.ds(h, TOK, stride=16), :].astype(BF16)
            send(*parts(j, r)[3], j, r)
            send(*parts(j, r)[0], j, r)
        return carry

    lax.fori_loop(0, 8, send_g, 0)
    cosine, sine = block_rope(near_ref, far_ref, s)
    loads[1].wait()
    v_wide[...] = v_raw[...].astype(F32).reshape(TOK * 8, HD)
    loads[2].wait()
    k_wide[...] = k_raw[...].astype(F32).reshape(TOK * 8, HD)

    def send_kv(t, carry):
        j = turns(t)
        rows = k_wide[pl.ds(j, TOK, stride=8), :]
        size = lax.rsqrt(jnp.mean(rows * rows, axis=1, keepdims=True) + EPS)
        kv_buf[0, j] = turn(rows * size * kg_ref[...], cosine, sine).astype(BF16)
        send(*parts(j, 0)[1], j, 0)
        kv_buf[1, j] = v_wide[pl.ds(j, TOK, stride=8), :].astype(BF16)
        send(*parts(j, 1)[1], j, 1)
        return carry

    lax.fori_loop(0, 8, send_kv, 0)
    loads[3].wait()
    q_wide[...] = q_raw[...].astype(F32).reshape(TOK * 16, HD)

    def send_q(t, carry):
        j = turns(t)
        for r in range(2):
            h = 2 * j + r
            rows = q_wide[pl.ds(h, TOK, stride=16), :]
            size = lax.rsqrt(jnp.mean(rows * rows, axis=1, keepdims=True) + EPS)
            q_buf[h] = (turn(rows * size * qg_ref[...], cosine, sine) * QMUL).astype(BF16)
            send(*parts(j, r)[2], j, r)
        return carry

    lax.fori_loop(0, 8, send_q, 0)

    def passing(kind, t):
        return pltpu.make_async_remote_copy(
            src_ref=kv_out.at[kind, t], dst_ref=kv_out.at[kind, t],
            send_sem=pass_send.at[t], recv_sem=pass_recv.at[t],
            device_id=(2 * z + 1 - core, s), device_id_type=MESH,
        )

    def arrival(kind, ref):
        return pltpu.make_async_copy(ref, ref, recv_sem.at[kind[0], kind[1]])

    def forward(i, carry):
        t = lax.rem(s + i, SEQ)
        arrival((1, t), kv_out.at[core, t]).wait()
        passing(core, t).start()
        return carry

    lax.fori_loop(0, SEQ, forward, 0)

    def finish(t, carry):
        arrival((0, t), g_out.at[t]).wait()
        arrival((2, t), q_out.at[t]).wait()
        arrival((3, t), seg_out.at[t]).wait()
        passing(core, t).wait_send()
        passing(1 - core, t).wait_recv()
        return carry

    lax.fori_loop(0, SEQ, finish, 0)

    def drain(j, carry):
        for r in range(2):
            for part in parts(j, r):
                sent(*part, j, r)
        return carry

    lax.fori_loop(0, 8, drain, 0)


def attend_kernel(
    q_ref, g_ref, kv_ref, seg_ref, near_ref, far_ref,
    dq_ref, dkv_ref, gain_ref,
    expo, pgrad, dk_acc, dv_acc, first_ref, dqt_acc,
):
    seg = seg_ref[...].reshape(SEQ, TOK)
    first = jnp.zeros((SEQ, TOK), F32)
    for d in range(1, 8):
        below = jnp.where(seg < d, 1.0, 0.0)
        count = jnp.sum(jnp.sum(below, axis=1, keepdims=True), axis=0, keepdims=True)
        first = jnp.where(seg == d, count, first)
    first_ref[...] = first.astype(jnp.int32)
    dk_acc[...] = jnp.zeros_like(dk_acc)
    dv_acc[...] = jnp.zeros_like(dv_acc)
    last = (((1,), (1,)), ((), ()))
    key_at = lax.broadcasted_iota(jnp.int32, (BLK, BLK), 0)
    query_at = lax.broadcasted_iota(jnp.int32, (BLK, BLK), 1)
    low_lane = lax.broadcasted_iota(jnp.int32, (1, TOK), 1)
    gain_q = jnp.zeros((8, HD), F32)

    for qi in range(NBLK):
        start = qi * BLK
        queries = q_ref[2 * qi:2 * qi + 2].reshape(BLK, HD)
        upstream = g_ref[2 * qi:2 * qi + 2].reshape(BLK, HD)
        firsts = jnp.concatenate(
            [first_ref[2 * qi:2 * qi + 1, :], first_ref[2 * qi + 1:2 * qi + 2, :]], axis=1
        )
        low = jnp.min(first[2 * qi:2 * qi + 1, :]).astype(jnp.int32)
        low = jnp.maximum(lax.div(low, BLK), max(0, qi - BAND + 1))

        def rows_of(kind, kb):
            return kv_ref[kind, pl.ds(2 * kb, 2)].reshape(BLK, HD)

        def scores(kb, diagonal, state):
            total, mixed = state
            slot = kb - max(0, qi - BAND + 1)
            st = lax.dot_general(rows_of(0, kb), queries, last, preferred_element_type=F32)
            dpt = lax.dot_general(rows_of(1, kb), upstream, last, preferred_element_type=F32)
            seen = key_at >= firsts - kb * BLK
            if diagonal:
                seen = seen & (key_at <= query_at)
            e = jnp.where(seen, jnp.exp2(st), 0.0)
            expo[slot] = e
            pgrad[slot] = dpt
            total = total + jnp.sum(e.reshape(BLK // 8, 8, BLK), axis=0)
            mixed = mixed + jnp.sum((e * dpt).reshape(BLK // 8, 8, BLK), axis=0)
            return total, mixed

        zero = jnp.zeros((8, BLK), F32)
        state = lax.fori_loop(
            low, qi, lambda kb, state: scores(kb, False, state), (zero, zero)
        )
        total, mixed = scores(qi, True, state)
        inv = 1.0 / jnp.sum(total, axis=0, keepdims=True)
        delta = jnp.sum(mixed, axis=0, keepdims=True) * inv
        dqt_acc[...] = jnp.zeros_like(dqt_acc)

        def grads(kb, carry):
            slot = kb - max(0, qi - BAND + 1)
            p = expo[slot] * inv
            ds = (p * (pgrad[slot] - delta)).astype(BF16)
            p = p.astype(BF16)
            rows = pl.ds(pl.multiple_of(kb * BLK, BLK), BLK)
            dv_acc[rows, :] += jnp.dot(p, upstream, preferred_element_type=F32)
            dk_acc[rows, :] += jnp.dot(ds, queries, preferred_element_type=F32)
            dqt_acc[...] += lax.dot_general(
                ds, rows_of(0, kb), (((0,), (0,)), ((), ())), preferred_element_type=F32
            )
            return carry

        lax.fori_loop(low, qi + 1, grads, 0)
        dq = dqt_acc[...] * SCALE
        for half in range(2):
            block = 2 * qi + half
            rows = dq[half * TOK:(half + 1) * TOK, :]
            dq_ref[block] = rows.astype(BF16)
            cosine, sine = block_rope(near_ref, far_ref, block)
            both = turn_back(rows, cosine, sine) * turn_back(
                q_ref[block].astype(F32), cosine, sine
            )
            gain_q = gain_q + jnp.sum(both.reshape(TOK // 8, 8, HD), axis=0)

    def keys_out(block, gain_k):
        rows = pl.ds(pl.multiple_of(block * TOK, TOK), TOK)
        dk = dk_acc[rows, :] * LN2
        dkv_ref[0, block] = dk.astype(BF16)
        dkv_ref[1, block] = dv_acc[rows, :].astype(BF16)
        cosine, sine = block_rope(near_ref, far_ref, block)
        both = turn_back(dk, cosine, sine) * turn_back(
            kv_ref[0, block].astype(F32), cosine, sine
        )
        return gain_k + jnp.sum(both.reshape(TOK // 8, 8, HD), axis=0)

    gain_k = lax.fori_loop(0, SEQ, keys_out, jnp.zeros((8, HD), F32))
    row = lax.broadcasted_iota(jnp.int32, (8, HD), 0)
    gain_ref[...] = jnp.where(
        row == 0,
        jnp.sum(gain_q, axis=0, keepdims=True),
        jnp.where(row == 1, jnp.sum(gain_k, axis=0, keepdims=True), 0.0),
    )


def scatter_kernel(
    dq_hbm, dkv_hbm, gain_ref,
    dq_out, dkv_out, gain_out,
    mate, own, mine, along_z, plane, z_sum,
    load_sem, send_sem, recv_sem, pass_send, pass_recv, zs, zr, ps, pr,
):
    dp, s, z, core = place()
    span = lax.rem(s, 2)
    j = lax.div(s, 2)
    slot_q = 2 * j + core
    slot_kv = core * 8 + j
    other = (2 * z + 1 - core, s)
    load = pltpu.make_async_copy(dkv_hbm.at[core], own, load_sem)
    load.start()
    barrier = greet(z, dp, s, core)

    def greet_z(i, carry):
        @pl.when(i != z)
        def _():
            pl.semaphore_signal(
                barrier, inc=1, device_id=(2 * i + core, s), device_id_type=MESH
            )

        return carry

    lax.fori_loop(0, SEQ, greet_z, 0)
    pl.semaphore_wait(barrier, 2 * SEQ - 1 + SEQ - 1)

    def swap(t):
        return pltpu.make_async_remote_copy(
            src_ref=dkv_hbm.at[1 - core, t], dst_ref=mate.at[t],
            send_sem=pass_send.at[t], recv_sem=pass_recv.at[t],
            device_id=other, device_id_type=MESH,
        )

    def along(i):
        return pltpu.make_async_remote_copy(
            src_ref=gain_ref, dst_ref=along_z.at[z], send_sem=zs.at[i], recv_sem=zr.at[z],
            device_id=(2 * i + core, s), device_id_type=MESH,
        )

    def across(i):
        return pltpu.make_async_remote_copy(
            src_ref=z_sum, dst_ref=plane.at[core * SEQ + s],
            send_sem=ps.at[i], recv_sem=pr.at[core * SEQ + s],
            device_id=(2 * z + lax.div(i, SEQ), lax.rem(i, SEQ)), device_id_type=MESH,
        )

    def copies(kind, src, dst, t):
        peer_dp = 2 * z + span
        me = (peer_dp == dp) & (t == s)
        slot = slot_q if kind == 0 else slot_kv
        remote = pltpu.make_async_remote_copy(
            src_ref=src, dst_ref=dst, send_sem=send_sem.at[kind, t],
            recv_sem=recv_sem.at[kind, slot], device_id=(peer_dp, t), device_id_type=MESH,
        )
        local = pltpu.make_async_copy(src, dst, recv_sem.at[kind, slot])
        return me, remote, local

    def parts(t):
        return ((0, dq_hbm.at[t], dq_out.at[slot_q]), (1, mine.at[t], dkv_out.at[slot_kv]))

    def send(kind, src, dst, t):
        me, remote, local = copies(kind, src, dst, t)

        @pl.when(me)
        def _():
            local.start()

        @pl.when(jnp.logical_not(me))
        def _():
            remote.start()

    def first(i, carry):
        @pl.when(i != z)
        def _():
            along(i).start()

        swap(lax.rem(s + i, SEQ)).start()
        return carry

    lax.fori_loop(0, SEQ, first, 0)
    along_z[z] = gain_ref[...]

    def send_q(i, carry):
        t = lax.rem(s + i, SEQ)
        send(*parts(t)[0], t)
        return carry

    lax.fori_loop(0, SEQ, send_q, 0)
    load.wait()

    def send_kv(i, carry):
        t = lax.rem(s + i, SEQ)
        swap(t).wait_recv()
        mine[t] = (own[t].astype(F32) + mate[t].astype(F32)).astype(BF16)
        send(*parts(t)[1], t)
        return carry

    lax.fori_loop(0, SEQ, send_kv, 0)

    def arrive_z(i, carry):
        @pl.when(i != z)
        def _():
            pltpu.make_async_copy(along_z.at[i], along_z.at[i], zr.at[i]).wait()

        return carry

    lax.fori_loop(0, SEQ, arrive_z, 0)
    z_sum[...] = jnp.sum(along_z[...], axis=0)

    def spread(i, carry):
        @pl.when(i != core * SEQ + s)
        def _():
            across(i).start()

        return carry

    lax.fori_loop(0, 2 * SEQ, spread, 0)
    plane[core * SEQ + s] = z_sum[...]

    def arrive_plane(i, carry):
        @pl.when(i != core * SEQ + s)
        def _():
            pltpu.make_async_copy(plane.at[i], plane.at[i], pr.at[i]).wait()

        return carry

    lax.fori_loop(0, 2 * SEQ, arrive_plane, 0)
    gain_out[...] = jnp.sum(plane[...], axis=0)

    def finish(t, carry):
        pltpu.make_async_copy(dq_out.at[t], dq_out.at[t], recv_sem.at[0, t]).wait()
        pltpu.make_async_copy(dkv_out.at[t], dkv_out.at[t], recv_sem.at[1, t]).wait()
        swap(t).wait_send()

        @pl.when(t != z)
        def _():
            along(t).wait_send()

        for part in parts(t):
            me, remote, local = copies(*part, t)

            @pl.when(jnp.logical_not(me))
            def _():
                remote.wait_send()

        return carry

    lax.fori_loop(0, SEQ, finish, 0)

    def drain(i, carry):
        @pl.when(i != core * SEQ + s)
        def _():
            across(i).wait_send()

        return carry

    lax.fori_loop(0, 2 * SEQ, drain, 0)


def norm_kernel(
    where_ref, dq_ref, dkv_ref, q_ref, k_ref, qg_ref, kg_ref, gain_ref, near_ref, far_ref,
    gq_ref, gk_ref, gv_ref, gqg_ref, gkg_ref,
    q_wide, k_wide, v_wide,
):
    cosine, sine = block_rope(near_ref, far_ref, where_ref[0])
    q_wide[...] = q_ref[...].astype(F32).reshape(TOK * 16, HD)
    k_wide[...] = k_ref[...].astype(F32).reshape(TOK * 8, HD)

    def back(wide, rows_at, upstream, gain):
        rows = wide[rows_at, :]
        size = lax.rsqrt(jnp.mean(rows * rows, axis=1, keepdims=True) + EPS)
        unit = rows * size
        slope = turn_back(upstream.astype(F32), cosine, sine) * gain
        wide[rows_at, :] = size * (slope - unit * jnp.mean(slope * unit, axis=1, keepdims=True))

    def queries(h, carry):
        back(q_wide, pl.ds(h, TOK, stride=16), dq_ref[h], qg_ref[...])
        return carry

    def keys(j, carry):
        back(k_wide, pl.ds(j, TOK, stride=8), dkv_ref[j], kg_ref[...])
        v_wide[pl.ds(j, TOK, stride=8), :] = dkv_ref[8 + j].astype(F32)
        return carry

    lax.fori_loop(0, 16, queries, 0)
    gq_ref[...] = q_wide[...].reshape(TOK, 16, HD).astype(BF16)
    lax.fori_loop(0, 8, keys, 0)
    gk_ref[...] = k_wide[...].reshape(TOK, 8, HD).astype(BF16)
    gv_ref[...] = v_wide[...].reshape(TOK, 8, HD).astype(BF16)
    gqg_ref[...] = gain_ref[0:1, :] / (qg_ref[...] * QMUL)
    gkg_ref[...] = gain_ref[1:2, :] / kg_ref[...]


def shape(dims, dtype):
    return jax.ShapeDtypeStruct(dims, dtype)


def body(q_pre, k_pre, values, grad_out, segment_ids, q_gain, k_gain):
    near, far = (jnp.asarray(table) for table in rope_tables())
    qg, kg = q_gain.reshape(1, HD), k_gain.reshape(1, HD)
    dma = pltpu.SemaphoreType.DMA
    tiles = (SEQ, TOK, HD)
    q_all, g_all, kv_all, seg_all = pl.pallas_call(
        gather_kernel,
        name="gather_heads",
        out_shape=(
            shape(tiles, BF16), shape(tiles, BF16), shape((2,) + tiles, BF16),
            shape((SEQ, 1, TOK), jnp.int32),
        ),
        in_specs=[ANY] * 4 + [VM] * 5,
        out_specs=(ANY,) * 4,
        scratch_shapes=[
            pltpu.VMEM((TOK, 16, HD), BF16), pltpu.VMEM((TOK, 8, HD), BF16),
            pltpu.VMEM((TOK, 8, HD), BF16), pltpu.VMEM((TOK, 16, HD), BF16),
            pltpu.VMEM((TOK * 16, HD), F32), pltpu.VMEM((TOK * 8, HD), F32),
            pltpu.VMEM((TOK * 8, HD), F32), pltpu.VMEM((TOK * 16, HD), F32),
            pltpu.VMEM(tiles, BF16), pltpu.VMEM(tiles, BF16),
            pltpu.VMEM((2, 8, TOK, HD), BF16),
            dma((4,)), dma((4, SEQ)), dma((4, SEQ)), dma((SEQ,)), dma((SEQ,)),
        ],
        compiler_params=pltpu.CompilerParams(
            collective_id=0, has_side_effects=True, vmem_limit_bytes=32 << 20
        ),
    )(q_pre[0], k_pre[0], values[0], grad_out[0], segment_ids, qg, kg, near, far)

    dq, dkv, gains = pl.pallas_call(
        attend_kernel,
        name="attend_back",
        out_shape=(shape(tiles, BF16), shape((2,) + tiles, BF16), shape((8, HD), F32)),
        in_specs=[VM] * 6,
        out_specs=(VM,) * 3,
        scratch_shapes=[
            pltpu.VMEM((BAND, BLK, BLK), F32), pltpu.VMEM((BAND, BLK, BLK), F32),
            pltpu.VMEM((TOTAL, HD), F32), pltpu.VMEM((TOTAL, HD), F32),
            pltpu.VMEM((SEQ, TOK), jnp.int32), pltpu.VMEM((BLK, HD), F32),
        ],
        compiler_params=pltpu.CompilerParams(vmem_limit_bytes=40 << 20),
    )(q_all, g_all, kv_all, seg_all, near, far)

    dq_back, dkv_back, gain_sums = pl.pallas_call(
        scatter_kernel,
        name="return_tokens",
        out_shape=(shape(tiles, BF16), shape(tiles, BF16), shape((8, HD), F32)),
        in_specs=[ANY, ANY, VM],
        out_specs=(ANY, ANY, VM),
        scratch_shapes=[
            pltpu.VMEM(tiles, BF16), pltpu.VMEM(tiles, BF16), pltpu.VMEM(tiles, BF16),
            pltpu.VMEM((SEQ, 8, HD), F32), pltpu.VMEM((2 * SEQ, 8, HD), F32),
            pltpu.VMEM((8, HD), F32),
            dma, dma((2, SEQ)), dma((2, SEQ)), dma((SEQ,)), dma((SEQ,)),
            dma((SEQ,)), dma((SEQ,)), dma((2 * SEQ,)), dma((2 * SEQ,)),
        ],
        compiler_params=pltpu.CompilerParams(
            collective_id=1, has_side_effects=True, vmem_limit_bytes=32 << 20
        ),
    )(dq, dkv, gains)

    where = lax.axis_index("seq").astype(jnp.int32).reshape(1)
    grad_q, grad_k, grad_v, grad_qg, grad_kg = pl.pallas_call(
        norm_kernel,
        name="norm_back",
        out_shape=(
            shape((TOK, 16, HD), BF16), shape((TOK, 8, HD), BF16), shape((TOK, 8, HD), BF16),
            shape((1, HD), F32), shape((1, HD), F32),
        ),
        in_specs=[pl.BlockSpec(memory_space=pltpu.SMEM)] + [VM] * 9,
        out_specs=(VM,) * 5,
        scratch_shapes=[
            pltpu.VMEM((TOK * 16, HD), F32), pltpu.VMEM((TOK * 8, HD), F32),
            pltpu.VMEM((TOK * 8, HD), F32),
        ],
        compiler_params=pltpu.CompilerParams(vmem_limit_bytes=32 << 20),
    )(where, dq_back, dkv_back, q_pre[0], k_pre[0], qg, kg, gain_sums, near, far)
    return (
        grad_q[None], grad_k[None], grad_v[None], grad_qg.reshape(HD), grad_kg.reshape(HD)
    )


def solution(mesh):
    tokens = P("dp", "seq", None, None)
    return jax.shard_map(
        body,
        mesh=mesh,
        in_specs=(tokens, tokens, tokens, tokens, P("dp", "seq"), P(), P()),
        out_specs=(tokens, tokens, tokens, P(), P()),
        check_vma=False,
    )
```

time: 310 us -> 91.7 us (0.30)
  blocking collectives: 139 us -> 0 us
  Pallas kernels: 0 us -> 84.3 us
  matrix products: 53.1 us -> 0 us
  waiting for transfers between devices: 34.4 us -> 0 us
  starting transfers between devices: 30.2 us -> 0 us
  local copies, waits for them, and re-layouts: 30.6 us -> 6.28 us
  other arithmetic: 19 us -> 0 us
    psum x1 -> x0, blocking collectives: 121 us -> none  [body(): gain_totals = lax.psum((query_gain_part, key_gain_part), ('dp', 'seq'))]
    pallas_call x0 -> x4, Pallas kernels: none -> 84.3 us  [the longest x1 32.2 us: body(): pl.pallas_call(gather_kernel, name='gather_heads', out_shape=(shape(tiles...]
    dot_general x70 -> x0, matrix products: 53.1 us -> none  [the longest x20 27.3 us: key_scores(): lax.dot_general(query_rows, key_rows, contract_last, preferred_element_ty...]
    all_to_all x7 -> x0, waiting for transfers between devices: 34.4 us -> none  [the longest x1 8.96 us: body(): lax.all_to_all(key_input.astype(jnp.bfloat16), 'seq', split_axis=0, conca...]
    all_to_all x7 -> x0, starting transfers between devices: 30.2 us -> none  [the longest x1 7.72 us: body(): lax.all_to_all(q_pre[0], 'seq', split_axis=1, concat_axis=0, tiled=True)]
    all_gather x1 -> x0, blocking collectives: 17.6 us -> none  [body(): segments = lax.all_gather(segment_ids, 'seq', axis=1, tiled=True)[0]]
    unnamed x40 -> x26, local copies, waits for them, and re-layouts: 14.1 us -> 6.28 us
    reduce_sum x12 -> x0, other arithmetic: 6.34 us -> none  [the longest x4 4.58 us: query_block(): delta = jnp.sum(upstream_rows.astype(jnp.float32) * outputs, axis=1)]
  transfers between devices with their start and end apart: 7 -> 0, of which waited for: 5 -> 0; matrix products, arithmetic and copies ran while one was open for 5% -> 0% of each run, Pallas kernels for 0% -> 0%
where the time goes in v1:
time: 91.7 us; the launch traced here: 91.3 us
  Pallas kernels  84.3 us (92%)
  local copies, waits for them, and re-layouts  6.28 us (7%)
    pallas_call x1, Pallas kernels, body(): pl.pallas_call(gather_kernel, name='gather_heads', out_shape=(shape(tiles...  32.2 us
    pallas_call x1, Pallas kernels, body(): pl.pallas_call(scatter_kernel, name='return_tokens', out_shape=(shape(til...  32 us
    pallas_call x1, Pallas kernels, body(): pl.pallas_call(attend_kernel, name='attend_back', out_shape=(shape(tiles,...  13.6 us
    pallas_call x1, Pallas kernels, body(): pl.pallas_call(norm_kernel, name='norm_back', out_shape=(shape((TOK, 16,...  6.5 us
    unnamed x26, local copies, waits for them, and re-layouts  6.28 us

profile of v1, /device:TPU:1, one launch (start us, length us, event | category | flops | bytes accessed | tf_op | source)
XLA Modules:
  0.0 91.3 jit_solution(517587345433006176)
XLA Ops:
  0.6 0.0 copy-start.10
  0.6 0.0 copy-start.11
  0.7 0.0 copy-start.12
  0.7 0.6 copy-done.10
  1.3 0.0 copy-done.11
  1.3 0.0 copy-done.12
  1.3 0.0 copy-start
  1.3 1.0 %copy-done = bf16[1,128,16,128]{3,2,1,0:T(8,128)(2,1)S(1)} copy-done((bf16[1,128,16,128]{3,2,1,0:T(8,128)(2,1)S(1)}, bf16[1,128,16,128]{3,2,1,0:T(8,128)(2,1)}, u32[]{:S(2)}) %copy-start) | copy-done | bytes 524312
  2.4 0.0 copy-start.2
  2.4 0.9 copy-done.2
  3.3 0.9 %copy-done.4 = bf16[1,128,8,128]{3,2,1,0:T(8,128)(2,1)S(1)} copy-done((bf16[1,128,8,128]{3,2,1,0:T(8,128)(2,1)S(1)}, bf16[1,128,8,128]{3,2,1,0:T(8,128)(2,1)}, u32[]{:S(2)}) %copy-start.4) | copy-done | bytes 262168
  4.2 1.0 %copy-done.6 = bf16[1,128,16,128]{3,2,1,0:T(8,128)(2,1)S(1)} copy-done((bf16[1,128,16,128]{3,2,1,0:T(8,128)(2,1)S(1)}, bf16[1,128,16,128]{3,2,1,0:T(8,128)(2,1)}, u32[]{:S(2)}) %copy-start.6) | copy-done | bytes 524312
  5.3 0.9 %copy-done.7 = bf16[1,128,8,128]{3,2,1,0:T(8,128)(2,1)S(1)} copy-done((bf16[1,128,8,128]{3,2,1,0:T(8,128)(2,1)S(1)}, bf16[1,128,8,128]{3,2,1,0:T(8,128)(2,1)}, u32[]{:S(2)}) %copy-start.7) | copy-done | bytes 262168
  6.2 0.7 copy-done.8
  6.9 32.2 %gather_heads.1 = (bf16[16,128,128]{2,1,0:T(8,128)(2,1)S(1)}, bf16[16,128,128]{2,1,0:T(8,128)(2,1)S(1)}, bf16[2,16,128,128]{3,2,1,0:T(8,128)(2,1)S(1)}, s32[16,1,128]{2,1,0:T(1,128)S(1)}) custom-call(bf16[128,16,128]{2,1,0:T(8,128)(2,1)S(1)} %bitcast.12, bf16[128,8,128]{2,1,0:T(8,128)(2,1)S(1)} %bitcast.14, bf16[128,8,128]{2,1,0:T(8,128)(2,1)S(1)} %bitcast.17, ...), custom_call_target="tpu_custom_call" | custom-call | tf_op jit(solution)/shard_map/gather_heads/pallas_call | solution.py:532
  39.1 0.0 copy-done.3
  39.2 0.0 copy-done.9
  39.2 13.6 %attend_back.1 = (bf16[16,128,128]{2,1,0:T(8,128)(2,1)S(1)}, bf16[2,16,128,128]{3,2,1,0:T(8,128)(2,1)S(1)}, f32[8,128]{1,0:T(8,128)S(1)}) custom-call(bf16[16,128,128]{2,1,0:T(8,128)(2,1)S(1)} %get-tuple-element.20.q_ref, bf16[16,128,128]{2,1,0:T(8,128)(2,1)S(1)} %get-tuple-element.21.g_ref, bf16[2,16,128,128]{3,2,1,0:T(8,128)(2,1)S(1)} %get-tuple-element.22.kv_ref, ...), custom_call_target="tpu_custom_call" | custom-call | tf_op jit(solution)/shard_map/attend_back/pallas_call | solution.py:555
  52.8 0.0 copy-start.1
  52.8 0.0 copy-start.5
  52.8 32.0 %return_tokens.1 = (bf16[16,128,128]{2,1,0:T(8,128)(2,1)S(1)}, bf16[16,128,128]{2,1,0:T(8,128)(2,1)S(1)}, f32[8,128]{1,0:T(8,128)S(1)}) custom-call(bf16[16,128,128]{2,1,0:T(8,128)(2,1)S(1)} %get-tuple-element.24.dq_hbm, bf16[2,16,128,128]{3,2,1,0:T(8,128)(2,1)S(1)} %get-tuple-element.25.dkv_hbm, f32[8,128]{1,0:T(8,128)S(1)} %get-tuple-element.26.gain_ref), custom_call_target="tpu_custom_call" | custom-call | tf_op jit(solution)/shard_map/return_tokens/pallas_call | solution.py:569
  84.8 0.0 copy-done.1
  84.8 0.0 copy-done.5
  84.8 6.5 %norm_back.1 = (bf16[128,16,128]{2,1,0:T(8,128)(2,1)}, bf16[128,8,128]{2,1,0:T(8,128)(2,1)}, bf16[128,8,128]{2,1,0:T(8,128)(2,1)}, f32[1,128]{1,0:T(1,128)}, f32[1,128]{1,0:T(1,128)}) custom-call(s32[1]{0:T(128)} %bitcast.where_ref, bf16[16,128,128]{2,1,0:T(8,128)(2,1)S(1)} %get-tuple-element.27.dq_ref, bf16[16,128,128]{2,1,0:T(8,128)(2,1)S(1)} %get-tuple-element.28.dkv_ref, ...), custom_call_target="tpu_custom_call" | custom-call | tf_op jit(solution)/shard_map/norm_back/pallas_call | solution.py:588
  (6 shorter events, 0.0 us)
Async XLA Ops:
  0.6 0.7 copy-start.10
  0.6 0.7 copy-start.11
  0.7 0.7 copy-start.12
  1.3 1.0 %copy-start = (bf16[1,128,16,128]{3,2,1,0:T(8,128)(2,1)S(1)}, bf16[1,128,16,128]{3,2,1,0:T(8,128)(2,1)}, u32[]{:S(2)}) copy-start(bf16[1,128,16,128]{3,2,1,0:T(8,128)(2,1)} %param.9) | copy-start | bytes 1572868
  2.4 0.9 copy-start.2
  3.3 0.9 %copy-start.4 = (bf16[1,128,8,128]{3,2,1,0:T(8,128)(2,1)S(1)}, bf16[1,128,8,128]{3,2,1,0:T(8,128)(2,1)}, u32[]{:S(2)}) copy-start(bf16[1,128,8,128]{3,2,1,0:T(8,128)(2,1)} %param.10) | copy-start | bytes 786436
  4.2 1.0 %copy-start.6 = (bf16[1,128,16,128]{3,2,1,0:T(8,128)(2,1)S(1)}, bf16[1,128,16,128]{3,2,1,0:T(8,128)(2,1)}, u32[]{:S(2)}) copy-start(bf16[1,128,16,128]{3,2,1,0:T(8,128)(2,1)} %param.12) | copy-start | bytes 1572868
  5.3 0.9 %copy-start.7 = (bf16[1,128,8,128]{3,2,1,0:T(8,128)(2,1)S(1)}, bf16[1,128,8,128]{3,2,1,0:T(8,128)(2,1)}, u32[]{:S(2)}) copy-start(bf16[1,128,8,128]{3,2,1,0:T(8,128)(2,1)} %param.11) | copy-start | bytes 786436
  6.2 0.7 copy-start.8
  6.9 32.2 %copy-start.3 = (f32[2,128,128]{2,1,0:T(8,128)S(1)}, f32[2,128,128]{2,1,0:T(8,128)}, u32[]{:S(2)}) copy-start(f32[2,128,128]{2,1,0:T(8,128)} %constant.8.clone.near_ref) | copy-start | bytes 393220
  6.9 32.2 %copy-start.9 = (f32[16,2,128]{2,1,0:T(2,128)S(1)}, f32[16,2,128]{2,1,0:T(2,128)}, u32[]{:S(2)}) copy-start(f32[16,2,128]{2,1,0:T(2,128)} %constant.9.clone.far_ref) | copy-start | bytes 49156
  52.8 32.0 %copy-start.1 = (bf16[1,128,16,128]{3,2,1,0:T(8,128)(2,1)S(1)}, bf16[1,128,16,128]{3,2,1,0:T(8,128)(2,1)}, u32[]{:S(2)}) copy-start(bf16[1,128,16,128]{3,2,1,0:T(8,128)(2,1)} %param.9) | copy-start | bytes 1572868
  52.8 32.0 %copy-start.5 = (bf16[1,128,8,128]{3,2,1,0:T(8,128)(2,1)S(1)}, bf16[1,128,8,128]{3,2,1,0:T(8,128)(2,1)}, u32[]{:S(2)}) copy-start(bf16[1,128,8,128]{3,2,1,0:T(8,128)(2,1)} %param.10) | copy-start | bytes 786436

commit v2 on v0

v2 whole, which is shorter than its diff:
```python
import jax
import jax.numpy as jnp
import numpy as np
from jax import lax
from jax.experimental import pallas as pl
from jax.experimental.pallas import tpu as pltpu
from jax.sharding import PartitionSpec as P

PRESCALE = 168
HD = 128
SEQ = 16
TOK = 128
TOTAL = SEQ * TOK
BLK = 256
NBLK = TOTAL // BLK
BAND = 5
EPS = 1e-6
ROPE_BASE = 1000000.0
ROPE_FACTOR = 8.0
SCALE = float(PRESCALE) ** (-0.5)
QMUL = SCALE * float(np.log2(np.e))
LN2 = float(np.log(2.0))
MESH = pl.DeviceIdType.MESH
F32 = jnp.float32
BF16 = jnp.bfloat16
ANY = pl.BlockSpec(memory_space=pl.ANY)
HBM = pl.BlockSpec(memory_space=pltpu.HBM)
VM = pl.BlockSpec(memory_space=pltpu.VMEM)


def rope_tables():
    half = HD // 2
    freqs = ROPE_BASE ** (-(np.arange(half, dtype=np.float64) * 2.0 / HD))
    freqs = np.concatenate([freqs, freqs])
    near = np.arange(TOK, dtype=np.float64)[:, None] / ROPE_FACTOR * freqs[None, :]
    far = np.arange(SEQ, dtype=np.float64)[:, None] * TOK / ROPE_FACTOR * freqs[None, :]
    return (
        np.stack([np.cos(near), np.sin(near)]).astype(np.float32),
        np.stack([np.cos(far), np.sin(far)], axis=1).astype(np.float32),
    )


def block_rope(near_ref, far_ref, block):
    far = far_ref[block]
    cb, sb = far[0:1, :], far[1:2, :]
    cosine = near_ref[0] * cb - near_ref[1] * sb
    sine = near_ref[1] * cb + near_ref[0] * sb
    lane = lax.broadcasted_iota(jnp.int32, (TOK, HD), 1)
    return cosine, jnp.where(lane < HD // 2, -sine, sine)


def turn(rows, cosine, sine):
    return rows * cosine + pltpu.roll(rows, HD // 2, 1) * sine


def turn_back(rows, cosine, sine):
    return rows * cosine - pltpu.roll(rows, HD // 2, 1) * sine


def place():
    dp = lax.axis_index("dp")
    s = lax.axis_index("seq")
    z = lax.div(dp, 2)
    return dp, s, z, lax.rem(dp, 2)


def fused_kernel(
    q_hbm, k_hbm, v_hbm, g_hbm, seg_hbm, qg_hbm, kg_hbm, near_hbm, far_hbm,
    dq_out, dkv_out, gain_out,
    q_raw, k_raw, v_raw, g_raw, seg_one, qg_ref, kg_ref, near_ref, far_ref,
    q_wide, k_wide, v_wide, g_wide, q_buf, g_buf, kv_buf,
    q_all, g_all, kv_all, seg_all, first_ref, inv_ref,
    expo, pgrad, dq_acc, dk_acc, dv_acc, gain_acc,
    dq_buf, dkv_buf, mate, mine, gain_one, along_z, plane, z_sum,
    load_sem, send_sem, recv_sem, pass_send, pass_recv,
    back_send, back_recv, swap_send, swap_recv, zs, zr, ps, pr,
):
    dp, s, z, core = place()
    j_own = lax.div(s, 2)
    span = lax.rem(s, 2)
    mate_at = (2 * z + 1 - core, s)
    loads = [
        pltpu.make_async_copy(src, dst, load_sem.at[i])
        for i, (src, dst) in enumerate(
            (
                (k_hbm, k_raw), (near_hbm, near_ref), (far_hbm, far_ref), (kg_hbm, kg_ref),
                (qg_hbm, qg_ref), (seg_hbm, seg_one), (q_hbm, q_raw), (v_hbm, v_raw),
                (g_hbm, g_raw),
            )
        )
    ]
    for copy in loads:
        copy.start()
    barrier = pltpu.get_barrier_semaphore()

    def greet(i, carry):
        @pl.when(i != core * SEQ + s)
        def _():
            pl.semaphore_signal(
                barrier, inc=1, device_id=(2 * z + lax.div(i, SEQ), lax.rem(i, SEQ)),
                device_id_type=MESH,
            )

        return carry

    def greet_z(i, carry):
        @pl.when(i != z)
        def _():
            pl.semaphore_signal(
                barrier, inc=1, device_id=(2 * i + core, s), device_id_type=MESH
            )

        return carry

    lax.fori_loop(0, 2 * SEQ, greet, 0)
    lax.fori_loop(0, SEQ, greet_z, 0)
    for copy in loads[:6]:
        copy.wait()
    cosine, sine = block_rope(near_ref, far_ref, s)
    k_wide[...] = k_raw[...].astype(F32).reshape(TOK * 8, HD)
    pl.semaphore_wait(barrier, 2 * SEQ - 1 + SEQ - 1)

    def is_me(j, r):
        return (2 * z + r == dp) & (2 * j + core == s)

    def outward(kind, src, dst, j, r):
        return pltpu.make_async_remote_copy(
            src_ref=src, dst_ref=dst, send_sem=send_sem.at[kind, 2 * j + r],
            recv_sem=recv_sem.at[kind, s], device_id=(2 * z + r, 2 * j + core),
            device_id_type=MESH,
        )

    def send(part, j, r):
        kind, src, dst = part
        me = is_me(j, r)

        @pl.when(me)
        def _():
            pltpu.make_async_copy(src, dst, recv_sem.at[kind, s]).start()

        @pl.when(jnp.logical_not(me))
        def _():
            outward(kind, src, dst, j, r).start()

    def part_of(kind, j, r):
        h = 2 * j + r
        if kind == 0:
            return (0, g_buf.at[h], g_all.at[s])
        if kind == 1:
            return (1, kv_buf.at[r, j], kv_all.at[r, s])
        if kind == 2:
            return (2, q_buf.at[h], q_all.at[s])
        return (3, seg_one, seg_all.at[s])

    def turns(t):
        return lax.rem(j_own + t, SEQ // 2)

    def send_k(t, carry):
        j = turns(t)
        rows = k_wide[pl.ds(j, TOK, stride=8), :]
        size = lax.rsqrt(jnp.mean(rows * rows, axis=1, keepdims=True) + EPS)
        kv_buf[0, j] = turn(rows * size * kg_ref[...], cosine, sine).astype(BF16)
        send(part_of(1, j, 0), j, 0)
        for r in range(2):
            send(part_of(3, j, r), j, r)
        return carry

    lax.fori_loop(0, 8, send_k, 0)
    loads[6].wait()
    q_wide[...] = q_raw[...].astype(F32).reshape(TOK * 16, HD)

    def send_q(t, carry):
        j = turns(t)
        for r in range(2):
            h = 2 * j + r
            rows = q_wide[pl.ds(h, TOK, stride=16), :]
            size = lax.rsqrt(jnp.mean(rows * rows, axis=1, keepdims=True) + EPS)
            q_buf[h] = (turn(rows * size * qg_ref[...], cosine, sine) * QMUL).astype(BF16)
            send(part_of(2, j, r), j, r)
        return carry

    lax.fori_loop(0, 8, send_q, 0)
    loads[7].wait()
    v_wide[...] = v_raw[...].astype(F32).reshape(TOK * 8, HD)

    def send_v(t, carry):
        j = turns(t)
        kv_buf[1, j] = v_wide[pl.ds(j, TOK, stride=8), :].astype(BF16)
        send(part_of(1, j, 1), j, 1)
        return carry

    lax.fori_loop(0, 8, send_v, 0)
    loads[8].wait()
    g_wide[...] = g_raw[...].astype(F32).reshape(TOK * 16, HD)

    def send_g(t, carry):
        j = turns(t)
        for r in range(2):
            h = 2 * j + r
            g_buf[h] = g_wide[pl.ds(h, TOK, stride=16), :].astype(BF16)
            send(part_of(0, j, r), j, r)
        return carry

    lax.fori_loop(0, 8, send_g, 0)

    def passing(kind, t):
        return pltpu.make_async_remote_copy(
            src_ref=kv_all.at[kind, t], dst_ref=kv_all.at[kind, t],
            send_sem=pass_send.at[t], recv_sem=pass_recv.at[t],
            device_id=mate_at, device_id_type=MESH,
        )

    def arrive(kind, t, ref):
        pltpu.make_async_copy(ref, ref, recv_sem.at[kind, t]).wait()

    def forward(i, carry):
        t = lax.rem(s + i, SEQ)
        arrive(1, t, kv_all.at[core, t])
        passing(core, t).start()
        return carry

    @pl.when(core == 0)
    def _():
        lax.fori_loop(0, SEQ, forward, 0)

    def got_first(t, carry):
        arrive(2, t, q_all.at[t])
        arrive(3, t, seg_all.at[t])

        @pl.when(core == 1)
        def _():
            passing(0, t).wait_recv()

        return carry

    lax.fori_loop(0, SEQ, got_first, 0)

    seg = seg_all[...].reshape(SEQ, TOK)
    first = jnp.zeros((SEQ, TOK), F32)
    for d in range(1, 8):
        below = jnp.where(seg < d, 1.0, 0.0)
        count = jnp.sum(jnp.sum(below, axis=1, keepdims=True), axis=0, keepdims=True)
        first = jnp.where(seg == d, count, first)
    first_ref[...] = first.astype(jnp.int32).reshape(SEQ, 1, TOK)
    dk_acc[...] = jnp.zeros_like(dk_acc)
    dv_acc[...] = jnp.zeros_like(dv_acc)
    gain_acc[...] = jnp.zeros_like(gain_acc)
    last = (((1,), (1,)), ((), ()))
    lead = (((0,), (0,)), ((), ()))

    def pair(ref, qi):
        return ref[pl.ds(2 * qi, 2)].reshape(BLK, HD)

    def keys_of(kind, kb):
        return kv_all[kind, pl.ds(2 * kb, 2)].reshape(BLK, HD)

    def fold(x):
        return jnp.sum(x.reshape(BLK // 8, 8, BLK), axis=0)

    def forward_block(i, carry):
        qi = turns(i)
        queries = pair(q_all, qi)
        firsts = jnp.concatenate([first_ref[2 * qi], first_ref[2 * qi + 1]], axis=1)
        key_at = lax.broadcasted_iota(jnp.int32, (BLK, BLK), 0)
        query_at = lax.broadcasted_iota(jnp.int32, (BLK, BLK), 1)
        total = jnp.zeros((8, BLK), F32)
        for d in range(BAND):
            kb = jnp.maximum(qi - d, 0)
            st = lax.dot_general(keys_of(0, kb), queries, last, preferred_element_type=F32)
            seen = key_at >= firsts - (qi - d) * BLK
            if d == 0:
                seen = seen & (key_at <= query_at)
            e = jnp.where(seen, jnp.exp2(st), 0.0)
            expo[qi, d] = e
            total = total + fold(e)
        inv_ref[qi] = 1.0 / jnp.sum(total, axis=0, keepdims=True)
        return carry

    lax.fori_loop(0, NBLK, forward_block, 0)

    @pl.when(core == 1)
    def _():
        lax.fori_loop(0, SEQ, forward, 0)

    def got_second(t, carry):
        arrive(0, t, g_all.at[t])

        @pl.when(core == 0)
        def _():
            passing(1, t).wait_recv()

        return carry

    lax.fori_loop(0, SEQ, got_second, 0)

    slot_q = 2 * j_own + core
    slot_kv = core * 8 + j_own

    def homeward(kind, src, dst, t):
        return pltpu.make_async_remote_copy(
            src_ref=src, dst_ref=dst, send_sem=back_send.at[kind, t],
            recv_sem=back_recv.at[kind, slot_q if kind == 0 else slot_kv],
            device_id=(2 * z + span, t), device_id_type=MESH,
        )

    def back_part(kind, t):
        if kind == 0:
            return (0, dq_buf.at[t], dq_out.at[slot_q])
        return (1, mine.at[t], dkv_out.at[slot_kv])

    def home(t):
        return (span == core) & (t == s)

    def send_back(part, t):
        kind, src, dst = part

        @pl.when(home(t))
        def _():
            pltpu.make_async_copy(
                src, dst, back_recv.at[kind, slot_q if kind == 0 else slot_kv]
            ).start()

        @pl.when(jnp.logical_not(home(t)))
        def _():
            homeward(kind, src, dst, t).start()

    def backward_block(i, carry):
        qi = turns(i)
        queries = pair(q_all, qi)
        upstream = pair(g_all, qi)
        inv = inv_ref[qi]
        mixed = jnp.zeros((8, BLK), F32)
        for d in range(BAND):
            kb = jnp.maximum(qi - d, 0)
            dpt = lax.dot_general(keys_of(1, kb), upstream, last, preferred_element_type=F32)
            pgrad[d] = dpt
            mixed = mixed + fold(expo[qi, d] * dpt)
        delta = jnp.sum(mixed, axis=0, keepdims=True) * inv
        dq = jnp.zeros((BLK, HD), F32)
        for d in range(BAND):
            kb = jnp.maximum(qi - d, 0)
            p = expo[qi, d] * inv
            ds = (p * (pgrad[d] - delta)).astype(BF16)
            p = p.astype(BF16)
            rows = pl.ds(pl.multiple_of(kb * BLK, BLK), BLK)
            dv_acc[rows, :] += jnp.dot(p, upstream, preferred_element_type=F32)
            dk_acc[rows, :] += jnp.dot(ds, queries, preferred_element_type=F32)
            dq = dq + lax.dot_general(ds, keys_of(0, kb), lead, preferred_element_type=F32)
        dq = dq * SCALE
        gain = gain_acc[...]
        for half in range(2):
            block = 2 * qi + half
            rows = dq[half * TOK:(half + 1) * TOK, :]
            dq_buf[block] = rows.astype(BF16)
            send_back(back_part(0, block), block)
            cb, sb = block_rope(near_ref, far_ref, block)
            both = turn_back(rows, cb, sb) * turn_back(q_all[block].astype(F32), cb, sb)
            gain = gain + jnp.sum(both.reshape(TOK // 8, 8, HD), axis=0)
        gain_acc[...] = gain
        return carry

    lax.fori_loop(0, NBLK, backward_block, 0)

    def swap(t):
        return pltpu.make_async_remote_copy(
            src_ref=dkv_buf.at[1 - core, t], dst_ref=mate.at[t],
            send_sem=swap_send.at[t], recv_sem=swap_recv.at[t],
            device_id=mate_at, device_id_type=MESH,
        )

    def keys_out(i, gain_k):
        block = lax.rem(s + i, SEQ)
        rows = pl.ds(pl.multiple_of(block * TOK, TOK), TOK)
        dk = dk_acc[rows, :] * LN2
        dkv_buf[0, block] = dk.astype(BF16)
        dkv_buf[1, block] = dv_acc[rows, :].astype(BF16)
        swap(block).start()
        cb, sb = block_rope(near_ref, far_ref, block)
        both = turn_back(dk, cb, sb) * turn_back(kv_all[0, block].astype(F32), cb, sb)
        return gain_k + jnp.sum(both.reshape(TOK // 8, 8, HD), axis=0)

    gain_k = lax.fori_loop(0, SEQ, keys_out, jnp.zeros((8, HD), F32))
    row = lax.broadcasted_iota(jnp.int32, (8, HD), 0)
    gain_one[...] = jnp.where(
        row == 0,
        jnp.sum(gain_acc[...], axis=0, keepdims=True),
        jnp.where(row == 1, jnp.sum(gain_k, axis=0, keepdims=True), 0.0),
    )

    def along(i):
        return pltpu.make_async_remote_copy(
            src_ref=gain_one, dst_ref=along_z.at[z], send_sem=zs.at[i], recv_sem=zr.at[z],
            device_id=(2 * i + core, s), device_id_type=MESH,
        )

    def across(i):
        return pltpu.make_async_remote_copy(
            src_ref=z_sum, dst_ref=plane.at[core * SEQ + s],
            send_sem=ps.at[i], recv_sem=pr.at[core * SEQ + s],
            device_id=(2 * z + lax.div(i, SEQ), lax.rem(i, SEQ)), device_id_type=MESH,
        )

    def gains_off(i, carry):
        @pl.when(i != z)
        def _():
            along(i).start()

        return carry

    lax.fori_loop(0, SEQ, gains_off, 0)
    along_z[z] = gain_one[...]

    def send_kv(i, carry):
        t = lax.rem(s + i, SEQ)
        swap(t).wait_recv()
        mine[t] = (dkv_buf[core, t].astype(F32) + mate[t].astype(F32)).astype(BF16)
        send_back(back_part(1, t), t)
        return carry

    lax.fori_loop(0, SEQ, send_kv, 0)

    def arrive_z(i, carry):
        @pl.when(i != z)
        def _():
            pltpu.make_async_copy(along_z.at[i], along_z.at[i], zr.at[i]).wait()

        return carry

    lax.fori_loop(0, SEQ, arrive_z, 0)
    z_sum[...] = jnp.sum(along_z[...], axis=0)

    def spread(i, carry):
        @pl.when(i != core * SEQ + s)
        def _():
            across(i).start()

        return carry

    lax.fori_loop(0, 2 * SEQ, spread, 0)
    plane[core * SEQ + s] = z_sum[...]

    def drain(j, carry):
        for r in range(2):
            for kind in (0, 2, 3):
                @pl.when(jnp.logical_not(is_me(j, r)))
                def _(kind=kind, r=r):
                    outward(*part_of(kind, j, r), j, r).wait_send()

            @pl.when(jnp.logical_not(is_me(j, r)))
            def _(r=r):
                outward(*part_of(1, j, r), j, r).wait_send()

        return carry

    lax.fori_loop(0, 8, drain, 0)

    def drain_back(t, carry):
        passing(core, t).wait_send()
        swap(t).wait_send()

        @pl.when(t != z)
        def _():
            along(t).wait_send()

        for kind in range(2):
            @pl.when(jnp.logical_not(home(t)))
            def _(kind=kind):
                homeward(*back_part(kind, t), t).wait_send()

        return carry

    lax.fori_loop(0, SEQ, drain_back, 0)

    def arrive_plane(i, carry):
        @pl.when(i != core * SEQ + s)
        def _():
            pltpu.make_async_copy(plane.at[i], plane.at[i], pr.at[i]).wait()
            across(i).wait_send()

        return carry

    lax.fori_loop(0, 2 * SEQ, arrive_plane, 0)
    gain_out[...] = jnp.sum(plane[...], axis=0)

    def arrive_back(t, carry):
        pltpu.make_async_copy(dq_out.at[t], dq_out.at[t], back_recv.at[0, t]).wait()
        pltpu.make_async_copy(dkv_out.at[t], dkv_out.at[t], back_recv.at[1, t]).wait()
        return carry

    lax.fori_loop(0, SEQ, arrive_back, 0)


def norm_kernel(
    where_ref, dq_ref, dkv_ref, q_ref, k_ref, qg_ref, kg_ref, gain_ref, near_ref, far_ref,
    gq_ref, gk_ref, gv_ref, gqg_ref, gkg_ref,
    q_wide, k_wide, q_new, k_new, v_new,
):
    cosine, sine = block_rope(near_ref, far_ref, where_ref[0])
    q_wide[...] = q_ref[...].astype(F32).reshape(TOK * 16, HD)
    k_wide[...] = k_ref[...].astype(F32).reshape(TOK * 8, HD)

    def back(wide, new, rows_at, upstream, gain):
        rows = wide[rows_at, :]
        size = lax.rsqrt(jnp.mean(rows * rows, axis=1, keepdims=True) + EPS)
        unit = rows * size
        slope = turn_back(upstream.astype(F32), cosine, sine) * gain
        new[rows_at, :] = size * (slope - unit * jnp.mean(slope * unit, axis=1, keepdims=True))

    for h in range(16):
        back(q_wide, q_new, pl.ds(h, TOK, stride=16), dq_ref[h], qg_ref[...])
    for j in range(8):
        back(k_wide, k_new, pl.ds(j, TOK, stride=8), dkv_ref[j], kg_ref[...])
        v_new[pl.ds(j, TOK, stride=8), :] = dkv_ref[8 + j].astype(F32)
    gq_ref[...] = q_new[...].reshape(TOK, 16, HD).astype(BF16)
    gk_ref[...] = k_new[...].reshape(TOK, 8, HD).astype(BF16)
    gv_ref[...] = v_new[...].reshape(TOK, 8, HD).astype(BF16)
    gqg_ref[...] = gain_ref[0:1, :] / (qg_ref[...] * QMUL)
    gkg_ref[...] = gain_ref[1:2, :] / kg_ref[...]


def shape(dims, dtype):
    return jax.ShapeDtypeStruct(dims, dtype)


def body(q_pre, k_pre, values, grad_out, segment_ids, q_gain, k_gain):
    near, far = (jnp.asarray(table) for table in rope_tables())
    qg, kg = q_gain.reshape(1, HD), k_gain.reshape(1, HD)
    dma = pltpu.SemaphoreType.DMA
    tiles = (SEQ, TOK, HD)
    dq_back, dkv_back, gain_sums = pl.pallas_call(
        fused_kernel,
        name="heads_and_back",
        out_shape=(shape(tiles, BF16), shape(tiles, BF16), shape((8, HD), F32)),
        in_specs=[HBM] * 9,
        out_specs=(ANY, ANY, VM),
        scratch_shapes=[
            pltpu.VMEM((TOK, 16, HD), BF16), pltpu.VMEM((TOK, 8, HD), BF16),
            pltpu.VMEM((TOK, 8, HD), BF16), pltpu.VMEM((TOK, 16, HD), BF16),
            pltpu.VMEM((1, TOK), jnp.int32), pltpu.VMEM((1, HD), F32), pltpu.VMEM((1, HD), F32),
            pltpu.VMEM((2, TOK, HD), F32), pltpu.VMEM((SEQ, 2, HD), F32),
            pltpu.VMEM((TOK * 16, HD), F32), pltpu.VMEM((TOK * 8, HD), F32),
            pltpu.VMEM((TOK * 8, HD), F32), pltpu.VMEM((TOK * 16, HD), F32),
            pltpu.VMEM(tiles, BF16), pltpu.VMEM(tiles, BF16),
            pltpu.VMEM((2, 8, TOK, HD), BF16),
            pltpu.VMEM(tiles, BF16), pltpu.VMEM(tiles, BF16), pltpu.VMEM((2,) + tiles, BF16),
            pltpu.VMEM((SEQ, 1, TOK), jnp.int32), pltpu.VMEM((SEQ, 1, TOK), jnp.int32),
            pltpu.VMEM((NBLK, 1, BLK), F32),
            pltpu.VMEM((NBLK, BAND, BLK, BLK), F32), pltpu.VMEM((BAND, BLK, BLK), F32),
            pltpu.VMEM((BLK, HD), F32), pltpu.VMEM((TOTAL, HD), F32),
            pltpu.VMEM((TOTAL, HD), F32), pltpu.VMEM((8, HD), F32),
            pltpu.VMEM(tiles, BF16), pltpu.VMEM((2,) + tiles, BF16),
            pltpu.VMEM(tiles, BF16), pltpu.VMEM(tiles, BF16),
            pltpu.VMEM((8, HD), F32), pltpu.VMEM((SEQ, 8, HD), F32),
            pltpu.VMEM((2 * SEQ, 8, HD), F32), pltpu.VMEM((8, HD), F32),
            dma((9,)), dma((4, SEQ)), dma((4, SEQ)), dma((SEQ,)), dma((SEQ,)),
            dma((2, SEQ)), dma((2, SEQ)), dma((SEQ,)), dma((SEQ,)),
            dma((SEQ,)), dma((SEQ,)), dma((2 * SEQ,)), dma((2 * SEQ,)),
        ],
        compiler_params=pltpu.CompilerParams(
            collective_id=0, has_side_effects=True, vmem_limit_bytes=48 << 20
        ),
    )(q_pre[0], k_pre[0], values[0], grad_out[0], segment_ids, qg, kg, near, far)

    where = lax.axis_index("seq").astype(jnp.int32).reshape(1)
    grad_q, grad_k, grad_v, grad_qg, grad_kg = pl.pallas_call(
        norm_kernel,
        name="norm_back",
        out_shape=(
            shape((TOK, 16, HD), BF16), shape((TOK, 8, HD), BF16), shape((TOK, 8, HD), BF16),
            shape((1, HD), F32), shape((1, HD), F32),
        ),
        in_specs=[pl.BlockSpec(memory_space=pltpu.SMEM)] + [VM] * 9,
        out_specs=(VM,) * 5,
        scratch_shapes=[
            pltpu.VMEM((TOK * 16, HD), F32), pltpu.VMEM((TOK * 8, HD), F32),
            pltpu.VMEM((TOK * 16, HD), F32), pltpu.VMEM((TOK * 8, HD), F32),
            pltpu.VMEM((TOK * 8, HD), F32),
        ],
        compiler_params=pltpu.CompilerParams(vmem_limit_bytes=32 << 20),
    )(where, dq_back, dkv_back, q_pre[0], k_pre[0], qg, kg, gain_sums, near, far)
    return (
        grad_q[None], grad_k[None], grad_v[None], grad_qg.reshape(HD), grad_kg.reshape(HD)
    )


def solution(mesh):
    tokens = P("dp", "seq", None, None)
    return jax.shard_map(
        body,
        mesh=mesh,
        in_specs=(tokens, tokens, tokens, tokens, P("dp", "seq"), P(), P()),
        out_specs=(tokens, tokens, tokens, P(), P()),
        check_vma=False,
    )
```

time: 310 us -> 78.6 us (0.25)
  blocking collectives: 139 us -> 0 us
  Pallas kernels: 0 us -> 71.9 us
  matrix products: 53.1 us -> 0 us
  waiting for transfers between devices: 34.4 us -> 0 us
  starting transfers between devices: 30.2 us -> 0 us
  local copies, waits for them, and re-layouts: 30.6 us -> 5.57 us
  other arithmetic: 19 us -> 0 us
    psum x1 -> x0, blocking collectives: 121 us -> none  [body(): gain_totals = lax.psum((query_gain_part, key_gain_part), ('dp', 'seq'))]
    pallas_call x0 -> x2, Pallas kernels: none -> 71.9 us  [the longest x1 67.7 us: body(): pl.pallas_call(fused_kernel, name='heads_and_back', out_shape=(shape(tile...]
    dot_general x70 -> x0, matrix products: 53.1 us -> none  [the longest x20 27.3 us: key_scores(): lax.dot_general(query_rows, key_rows, contract_last, preferred_element_ty...]
    all_to_all x7 -> x0, waiting for transfers between devices: 34.4 us -> none  [the longest x1 8.96 us: body(): lax.all_to_all(key_input.astype(jnp.bfloat16), 'seq', split_axis=0, conca...]
    all_to_all x7 -> x0, starting transfers between devices: 30.2 us -> none  [the longest x1 7.72 us: body(): lax.all_to_all(q_pre[0], 'seq', split_axis=1, concat_axis=0, tiled=True)]
    all_gather x1 -> x0, blocking collectives: 17.6 us -> none  [body(): segments = lax.all_gather(segment_ids, 'seq', axis=1, tiled=True)[0]]
    unnamed x40 -> x18, local copies, waits for them, and re-layouts: 14.1 us -> 5.57 us
    reduce_sum x12 -> x0, other arithmetic: 6.34 us -> none  [the longest x4 4.58 us: query_block(): delta = jnp.sum(upstream_rows.astype(jnp.float32) * outputs, axis=1)]
  transfers between devices with their start and end apart: 7 -> 0, of which waited for: 5 -> 0; matrix products, arithmetic and copies ran while one was open for 5% -> 0% of each run, Pallas kernels for 0% -> 0%
where the time goes in v2:
time: 78.6 us; the launch traced here: 78.2 us
  Pallas kernels  71.9 us (91%)
  local copies, waits for them, and re-layouts  5.57 us (7%)
    pallas_call x1, Pallas kernels, body(): pl.pallas_call(fused_kernel, name='heads_and_back', out_shape=(shape(tile...  67.7 us
    unnamed x18, local copies, waits for them, and re-layouts  5.57 us
    pallas_call x1, Pallas kernels, body(): pl.pallas_call(norm_kernel, name='norm_back', out_shape=(shape((TOK, 16,...  4.21 us

profile of v2, /device:TPU:1, one launch (start us, length us, event | category | flops | bytes accessed | tf_op | source)
XLA Modules:
  0.0 78.2 jit_solution(1022986066316236697)
XLA Ops:
  0.6 0.0 copy-start.5
  0.7 0.0 copy-start.6
  0.7 0.0 copy-start.7
  0.7 0.0 copy-start.8
  0.7 0.7 copy-done.5
  1.4 0.0 copy-done.6
  1.4 0.0 copy-done.7
  1.4 0.0 copy-done.8
  1.4 0.0 copy-start
  1.4 1.0 %copy-done = bf16[1,128,16,128]{3,2,1,0:T(8,128)(2,1)S(1)} copy-done((bf16[1,128,16,128]{3,2,1,0:T(8,128)(2,1)S(1)}, bf16[1,128,16,128]{3,2,1,0:T(8,128)(2,1)}, u32[]{:S(2)}) %copy-start) | copy-done | bytes 524312
  2.4 0.0 copy-start.1
  2.4 0.9 %copy-done.1 = bf16[1,128,8,128]{3,2,1,0:T(8,128)(2,1)S(1)} copy-done((bf16[1,128,8,128]{3,2,1,0:T(8,128)(2,1)S(1)}, bf16[1,128,8,128]{3,2,1,0:T(8,128)(2,1)}, u32[]{:S(2)}) %copy-start.1) | copy-done | bytes 262168
  3.4 0.0 copy-start.2
  3.4 1.0 %copy-done.2 = bf16[1,128,16,128]{3,2,1,0:T(8,128)(2,1)S(1)} copy-done((bf16[1,128,16,128]{3,2,1,0:T(8,128)(2,1)S(1)}, bf16[1,128,16,128]{3,2,1,0:T(8,128)(2,1)}, u32[]{:S(2)}) %copy-start.2) | copy-done | bytes 524312
  4.4 0.0 copy-start.3
  4.4 0.9 %copy-done.3 = f32[2,128,128]{2,1,0:T(8,128)S(1)} copy-done((f32[2,128,128]{2,1,0:T(8,128)S(1)}, f32[2,128,128]{2,1,0:T(8,128)}, u32[]{:S(2)}) %copy-start.3) | copy-done | bytes 131096
  5.3 0.0 copy-start.4
  5.3 0.9 %copy-done.4 = bf16[1,128,8,128]{3,2,1,0:T(8,128)(2,1)S(1)} copy-done((bf16[1,128,8,128]{3,2,1,0:T(8,128)(2,1)S(1)}, bf16[1,128,8,128]{3,2,1,0:T(8,128)(2,1)}, u32[]{:S(2)}) %copy-start.4) | copy-done | bytes 262168
  6.3 67.7 %heads_and_back.1 = (bf16[16,128,128]{2,1,0:T(8,128)(2,1)S(1)}, bf16[16,128,128]{2,1,0:T(8,128)(2,1)S(1)}, f32[8,128]{1,0:T(8,128)S(1)}) custom-call(bf16[128,16,128]{2,1,0:T(8,128)(2,1)S(1)} %bitcast.12, bf16[128,8,128]{2,1,0:T(8,128)(2,1)S(1)} %bitcast.14, bf16[128,8,128]{2,1,0:T(8,128)(2,1)S(1)} %bitcast.17, bf16[128,16,128]{2,1,0:T(8,128)(2,1)S(1)} %bitcast.16, ...), custom_call_target="tpu_custom_call" | custom-call | tf_op jit(solution)/shard_map/heads_and_back/pallas_call | solution.py:530
  74.0 4.2 %norm_back.1 = (bf16[128,16,128]{2,1,0:T(8,128)(2,1)}, bf16[128,8,128]{2,1,0:T(8,128)(2,1)}, bf16[128,8,128]{2,1,0:T(8,128)(2,1)}, f32[1,128]{1,0:T(1,128)}, f32[1,128]{1,0:T(1,128)}) custom-call(s32[1]{0:T(128)} %bitcast.where_ref, bf16[16,128,128]{2,1,0:T(8,128)(2,1)S(1)} %get-tuple-element.13.dq_ref, bf16[16,128,128]{2,1,0:T(8,128)(2,1)S(1)} %get-tuple-element.14.dkv_ref, ...), custom_call_target="tpu_custom_call" | custom-call | tf_op jit(solution)/shard_map/norm_back/pallas_call | solution.py:565
Async XLA Ops:
  0.6 0.7 copy-start.5
  0.7 0.7 copy-start.6
  0.7 0.7 copy-start.7
  0.7 0.7 copy-start.8
  1.4 1.0 %copy-start = (bf16[1,128,16,128]{3,2,1,0:T(8,128)(2,1)S(1)}, bf16[1,128,16,128]{3,2,1,0:T(8,128)(2,1)}, u32[]{:S(2)}) copy-start(bf16[1,128,16,128]{3,2,1,0:T(8,128)(2,1)} %param.9) | copy-start | bytes 1572868
  2.4 0.9 %copy-start.1 = (bf16[1,128,8,128]{3,2,1,0:T(8,128)(2,1)S(1)}, bf16[1,128,8,128]{3,2,1,0:T(8,128)(2,1)}, u32[]{:S(2)}) copy-start(bf16[1,128,8,128]{3,2,1,0:T(8,128)(2,1)} %param.10) | copy-start | bytes 786436
  3.4 1.0 %copy-start.2 = (bf16[1,128,16,128]{3,2,1,0:T(8,128)(2,1)S(1)}, bf16[1,128,16,128]{3,2,1,0:T(8,128)(2,1)}, u32[]{:S(2)}) copy-start(bf16[1,128,16,128]{3,2,1,0:T(8,128)(2,1)} %param.12) | copy-start | bytes 1572868
  4.4 0.9 %copy-start.3 = (f32[2,128,128]{2,1,0:T(8,128)S(1)}, f32[2,128,128]{2,1,0:T(8,128)}, u32[]{:S(2)}) copy-start(f32[2,128,128]{2,1,0:T(8,128)} %constant.8.clone.near_hbm.near_ref) | copy-start | bytes 393220
  5.3 0.9 %copy-start.4 = (bf16[1,128,8,128]{3,2,1,0:T(8,128)(2,1)S(1)}, bf16[1,128,8,128]{3,2,1,0:T(8,128)(2,1)}, u32[]{:S(2)}) copy-start(bf16[1,128,8,128]{3,2,1,0:T(8,128)(2,1)} %param.11) | copy-start | bytes 786436

commit v3 on v2

v3 whole, which is shorter than its diff:
```python
import jax
import jax.numpy as jnp
import numpy as np
from jax import lax
from jax.experimental import pallas as pl
from jax.experimental.pallas import tpu as pltpu
from jax.sharding import PartitionSpec as P

PRESCALE = 168
HD = 128
SEQ = 16
TOK = 128
TOTAL = SEQ * TOK
BLK = 256
NBLK = TOTAL // BLK
BAND = 5
EPS = 1e-6
ROPE_BASE = 1000000.0
ROPE_FACTOR = 8.0
SCALE = float(PRESCALE) ** (-0.5)
QMUL = SCALE * float(np.log2(np.e))
LN2 = float(np.log(2.0))
MESH = pl.DeviceIdType.MESH
F32 = jnp.float32
BF16 = jnp.bfloat16
ANY = pl.BlockSpec(memory_space=pl.ANY)
HBM = pl.BlockSpec(memory_space=pltpu.HBM)
VM = pl.BlockSpec(memory_space=pltpu.VMEM)


def rope_tables():
    half = HD // 2
    freqs = ROPE_BASE ** (-(np.arange(half, dtype=np.float64) * 2.0 / HD))
    freqs = np.concatenate([freqs, freqs])
    near = np.arange(TOK, dtype=np.float64)[:, None] / ROPE_FACTOR * freqs[None, :]
    far = np.arange(SEQ, dtype=np.float64)[:, None] * TOK / ROPE_FACTOR * freqs[None, :]
    return (
        np.stack([np.cos(near), np.sin(near)]).astype(np.float32),
        np.stack([np.cos(far), np.sin(far)], axis=1).astype(np.float32),
    )


def block_rope(near_ref, far_ref, block):
    far = far_ref[block]
    cb, sb = far[0:1, :], far[1:2, :]
    cosine = near_ref[0] * cb - near_ref[1] * sb
    sine = near_ref[1] * cb + near_ref[0] * sb
    lane = lax.broadcasted_iota(jnp.int32, (TOK, HD), 1)
    return cosine, jnp.where(lane < HD // 2, -sine, sine)


def turn(rows, cosine, sine):
    return rows * cosine + pltpu.roll(rows, HD // 2, 1) * sine


def turn_back(rows, cosine, sine):
    return rows * cosine - pltpu.roll(rows, HD // 2, 1) * sine


def place():
    dp = lax.axis_index("dp")
    s = lax.axis_index("seq")
    z = lax.div(dp, 2)
    return dp, s, z, lax.rem(dp, 2)


def fused_kernel(
    q_hbm, k_hbm, v_hbm, g_hbm, seg_hbm, qg_hbm, kg_hbm, near_hbm, far_hbm,
    dq_out, dkv_out, gain_out,
    q_raw, k_raw, v_raw, g_raw, seg_one, qg_ref, kg_ref, near_ref, far_ref,
    q_wide, k_wide, v_wide, g_wide, q_buf, g_buf, kv_buf,
    q_all, g_all, kv_all, seg_all, first_ref, cos_all, sin_all, q_unit, k_unit,
    expo, prob, pgrad, dq_acc, gain_acc,
    dq_buf, dkv_buf, mate, mine, gain_one, stages,
    load_sem, send_sem, recv_sem, pass_send, pass_recv, pass_got,
    back_send, back_recv, swap_send, swap_recv, stage_send, stage_recv,
):
    dp, s, z, core = place()
    j_own = lax.div(s, 2)
    span = lax.rem(s, 2)
    mate_at = (2 * z + 1 - core, s)
    loads = [
        pltpu.make_async_copy(src, dst, load_sem.at[i])
        for i, (src, dst) in enumerate(
            (
                (k_hbm, k_raw), (near_hbm, near_ref), (far_hbm, far_ref), (kg_hbm, kg_ref),
                (qg_hbm, qg_ref), (seg_hbm, seg_one), (q_hbm, q_raw), (v_hbm, v_raw),
                (g_hbm, g_raw),
            )
        )
    ]
    for copy in loads:
        copy.start()
    barrier = pltpu.get_barrier_semaphore()

    def greet(i, carry):
        @pl.when(i != core * SEQ + s)
        def _():
            pl.semaphore_signal(
                barrier, inc=1, device_id=(2 * z + lax.div(i, SEQ), lax.rem(i, SEQ)),
                device_id_type=MESH,
            )

        return carry

    x_at, y_at = lax.rem(s, 4), lax.div(s, 4)
    z_low, z_high = lax.rem(z, 2), lax.div(z, 2)

    def member(stage, i):
        if stage == 0:
            return (2 * z + lax.rem(i, 2), 4 * y_at + lax.div(i, 2))
        if stage == 1:
            return (2 * (2 * z_high + lax.rem(i, 2)) + core, 4 * lax.div(i, 2) + x_at)
        return (2 * (2 * i + z_low) + core, s)

    rank = (2 * x_at + core, 2 * y_at + z_low, z_high)

    def greet_low(i, carry):
        pl.semaphore_signal(
            barrier, inc=1, device_id=member(1, 2 * i + 1 - z_low), device_id_type=MESH
        )
        return carry

    def greet_high(i, carry):
        @pl.when(i != z_high)
        def _():
            pl.semaphore_signal(barrier, inc=1, device_id=member(2, i), device_id_type=MESH)

        return carry

    lax.fori_loop(0, 2 * SEQ, greet, 0)
    lax.fori_loop(0, 4, greet_low, 0)
    lax.fori_loop(0, 8, greet_high, 0)
    for copy in loads[:6]:
        copy.wait()
    cosine, sine = block_rope(near_ref, far_ref, s)
    k_wide[...] = k_raw[...].astype(F32).reshape(TOK * 8, HD)
    pl.semaphore_wait(barrier, 2 * SEQ - 1 + 4 + 7)

    def is_me(j, r):
        return (2 * z + r == dp) & (2 * j + core == s)

    def landing(kind):
        return recv_sem.at[kind] if kind != 1 else pass_got.at[s]

    def outward(kind, src, dst, j, r):
        return pltpu.make_async_remote_copy(
            src_ref=src, dst_ref=dst, send_sem=send_sem.at[kind], recv_sem=landing(kind),
            device_id=(2 * z + r, 2 * j + core), device_id_type=MESH,
        )

    def send(part, j, r):
        kind, src, dst = part
        me = is_me(j, r)

        @pl.when(me)
        def _():
            pltpu.make_async_copy(src, dst, landing(kind)).start()

        @pl.when(jnp.logical_not(me))
        def _():
            outward(kind, src, dst, j, r).start()

    def part_of(kind, j, r):
        h = 2 * j + r
        if kind == 0:
            return (0, g_buf.at[h], g_all.at[s])
        if kind == 1:
            return (1, kv_buf.at[r, j], kv_all.at[r, s])
        if kind == 2:
            return (2, q_buf.at[h], q_all.at[s])
        return (3, seg_one, seg_all.at[s])

    def turns(t):
        return lax.rem(j_own + t, SEQ // 2)

    def send_k(t, carry):
        j = turns(t)
        rows = k_wide[pl.ds(j, TOK, stride=8), :]
        size = lax.rsqrt(jnp.mean(rows * rows, axis=1, keepdims=True) + EPS)
        kv_buf[0, j] = turn(rows * size * kg_ref[...], cosine, sine).astype(BF16)
        send(part_of(1, j, 0), j, 0)
        for r in range(2):
            send(part_of(3, j, r), j, r)
        return carry

    lax.fori_loop(0, 8, send_k, 0)
    loads[6].wait()
    q_wide[...] = q_raw[...].astype(F32).reshape(TOK * 16, HD)

    def send_q(t, carry):
        j = turns(t)
        for r in range(2):
            h = 2 * j + r
            rows = q_wide[pl.ds(h, TOK, stride=16), :]
            size = lax.rsqrt(jnp.mean(rows * rows, axis=1, keepdims=True) + EPS)
            q_buf[h] = (turn(rows * size * qg_ref[...], cosine, sine) * QMUL).astype(BF16)
            send(part_of(2, j, r), j, r)
        return carry

    lax.fori_loop(0, 8, send_q, 0)
    loads[8].wait()
    g_wide[...] = g_raw[...].astype(F32).reshape(TOK * 16, HD)

    def send_g(t, carry):
        j = turns(t)
        for r in range(2):
            h = 2 * j + r
            g_buf[h] = g_wide[pl.ds(h, TOK, stride=16), :].astype(BF16)
            send(part_of(0, j, r), j, r)
        return carry

    lax.fori_loop(0, 8, send_g, 0)

    loads[7].wait()
    v_wide[...] = v_raw[...].astype(F32).reshape(TOK * 8, HD)

    def send_v(t, carry):
        j = turns(t)
        kv_buf[1, j] = v_wide[pl.ds(j, TOK, stride=8), :].astype(BF16)
        send(part_of(1, j, 1), j, 1)
        return carry

    lax.fori_loop(0, 8, send_v, 0)
    def passing(kind, t):
        return pltpu.make_async_remote_copy(
            src_ref=kv_all.at[kind, t], dst_ref=kv_all.at[kind, t],
            send_sem=pass_send, recv_sem=pass_recv,
            device_id=mate_at, device_id_type=MESH,
        )

    def wait_on(ref, sem):
        pltpu.make_async_copy(ref, ref, sem).wait()

    def forward(i, carry):
        t = lax.rem(s + i, SEQ)
        wait_on(kv_all.at[core, t], pass_got.at[t])
        passing(core, t).start()
        return carry

    def tables(t, carry):
        cb, sb = block_rope(near_ref, far_ref, t)
        cos_all[t] = cb
        sin_all[t] = sb
        return carry

    lax.fori_loop(0, SEQ, tables, 0)

    @pl.when(core == 0)
    def _():
        lax.fori_loop(0, SEQ, forward, 0)

    wait_on(q_all, recv_sem.at[2])
    wait_on(seg_all, recv_sem.at[3])

    @pl.when(core == 1)
    def _():
        wait_on(kv_all.at[0], pass_recv)

    seg = seg_all[...].reshape(SEQ, TOK)
    first = jnp.zeros((SEQ, TOK), F32)
    for d in range(1, 8):
        below = jnp.where(seg < d, 1.0, 0.0)
        count = jnp.sum(jnp.sum(below, axis=1, keepdims=True), axis=0, keepdims=True)
        first = jnp.where(seg == d, count, first)
    first_ref[...] = first.astype(jnp.int32).reshape(SEQ, 1, TOK)
    gain_acc[...] = jnp.zeros_like(gain_acc)
    last = (((1,), (1,)), ((), ()))
    lead = (((0,), (0,)), ((), ()))

    def pair(ref, qi):
        return ref[pl.ds(2 * qi, 2)].reshape(BLK, HD)

    def keys_of(kind, kb):
        return kv_all[kind, pl.ds(2 * kb, 2)].reshape(BLK, HD)

    def fold(x):
        return jnp.sum(x.reshape(BLK // 8, 8, BLK), axis=0)

    def by_queries(i, run):
        qi = turns(i)
        for count in range(1, BAND + 1):
            fits = (qi >= BAND - 1) if count == BAND else (qi == count - 1)

            @pl.when(fits)
            def _(count=count):
                run(qi, count)

    def by_keys(i, run):
        kb = turns(i)
        for count in range(1, BAND + 1):
            fits = (kb <= NBLK - BAND) if count == BAND else (kb == NBLK - count)

            @pl.when(fits)
            def _(count=count):
                run(kb, count)

    def forward_block(qi, count):
        queries = pair(q_all, qi)
        firsts = jnp.concatenate([first_ref[2 * qi], first_ref[2 * qi + 1]], axis=1)
        key_at = lax.broadcasted_iota(jnp.int32, (BLK, BLK), 0)
        query_at = lax.broadcasted_iota(jnp.int32, (BLK, BLK), 1)
        total = jnp.zeros((8, BLK), F32)
        for d in range(count):
            st = lax.dot_general(keys_of(0, qi - d), queries, last, preferred_element_type=F32)
            seen = key_at >= firsts - (qi - d) * BLK
            if d == 0:
                seen = seen & (key_at <= query_at)
            e = jnp.where(seen, jnp.exp2(st), 0.0)
            expo[d] = e
            total = total + fold(e)
        inv = 1.0 / jnp.sum(total, axis=0, keepdims=True)
        for d in range(count):
            prob[qi, d] = (expo[d] * inv).astype(BF16)

    def forward_step(i, carry):
        by_queries(i, forward_block)
        return carry

    lax.fori_loop(0, NBLK, forward_step, 0)

    def units(t, carry):
        cb, sb = cos_all[t], sin_all[t]
        q_unit[t] = turn_back(q_all[t].astype(F32), cb, sb)
        k_unit[t] = turn_back(kv_all[0, t].astype(F32), cb, sb)
        return carry

    lax.fori_loop(0, SEQ, units, 0)
    wait_on(g_all, recv_sem.at[0])

    def swap(kind, t):
        return pltpu.make_async_remote_copy(
            src_ref=dkv_buf.at[kind, t], dst_ref=mate.at[t],
            send_sem=swap_send, recv_sem=swap_recv.at[t],
            device_id=mate_at, device_id_type=MESH,
        )

    def value_block(kb, count):
        dv = jnp.dot(prob[kb, 0], pair(g_all, kb), preferred_element_type=F32)
        for d in range(1, count):
            dv = dv + jnp.dot(prob[kb + d, d], pair(g_all, kb + d), preferred_element_type=F32)
        dkv_buf[1, pl.ds(2 * kb, 2)] = dv.astype(BF16).reshape(2, TOK, HD)

    def value_step(i, carry):
        by_keys(i, value_block)
        kb = turns(i)

        @pl.when(core == 0)
        def _():
            swap(1, 2 * kb).start()
            swap(1, 2 * kb + 1).start()

        @pl.when(core == 1)
        def _():
            forward(2 * i, 0)
            forward(2 * i + 1, 0)

        return carry

    lax.fori_loop(0, NBLK, value_step, 0)

    @pl.when(core == 0)
    def _():
        wait_on(kv_all.at[1], pass_recv)

    slot_q = 2 * j_own + core
    slot_kv = core * 8 + j_own

    def homeward(kind, src, dst, t):
        return pltpu.make_async_remote_copy(
            src_ref=src, dst_ref=dst, send_sem=back_send.at[kind], recv_sem=back_recv.at[kind],
            device_id=(2 * z + span, t), device_id_type=MESH,
        )

    def back_part(kind, t):
        if kind == 0:
            return (0, dq_buf.at[t], dq_out.at[slot_q])
        return (1, mine.at[t], dkv_out.at[slot_kv])

    def home(t):
        return (span == core) & (t == s)

    def send_back(part, t):
        kind, src, dst = part

        @pl.when(home(t))
        def _():
            pltpu.make_async_copy(src, dst, back_recv.at[kind]).start()

        @pl.when(jnp.logical_not(home(t)))
        def _():
            homeward(kind, src, dst, t).start()

    def settle(kind, t):
        swap(kind, t).wait_recv()
        mine[t] = (dkv_buf[kind, t].astype(F32) + mate[t].astype(F32)).astype(BF16)
        send_back(back_part(1, t), t)

    def backward_block(qi, count):
        upstream = pair(g_all, qi)
        mixed = jnp.zeros((8, BLK), F32)
        for d in range(count):
            dpt = lax.dot_general(
                keys_of(1, qi - d), upstream, last, preferred_element_type=F32
            )
            pgrad[d] = dpt
            mixed = mixed + fold(prob[qi, d].astype(F32) * dpt)
        delta = jnp.sum(mixed, axis=0, keepdims=True)
        dq = jnp.zeros((BLK, HD), F32)
        for d in range(count):
            ds = (prob[qi, d].astype(F32) * (pgrad[d] - delta)).astype(BF16)
            prob[qi, d] = ds
            dq = dq + lax.dot_general(ds, keys_of(0, qi - d), lead, preferred_element_type=F32)
        dq_acc[...] = dq * SCALE

    def backward_step(i, carry):
        by_queries(i, backward_block)
        qi = turns(i)
        gain = gain_acc[...]
        for half in range(2):
            block = 2 * qi + half
            rows = dq_acc[half * TOK:(half + 1) * TOK, :]
            dq_buf[block] = rows.astype(BF16)
            send_back(back_part(0, block), block)
            both = turn_back(rows, cos_all[block], sin_all[block]) * q_unit[block]
            gain = gain + jnp.sum(both.reshape(TOK // 8, 8, HD), axis=0)
        gain_acc[...] = gain

        @pl.when(core == 1)
        def _():
            settle(1, 2 * qi)
            settle(1, 2 * qi + 1)

        return carry

    lax.fori_loop(0, NBLK, backward_step, 0)

    def key_block(kb, count):
        dk = jnp.dot(prob[kb, 0], pair(q_all, kb), preferred_element_type=F32)
        for d in range(1, count):
            dk = dk + jnp.dot(prob[kb + d, d], pair(q_all, kb + d), preferred_element_type=F32)
        dq_acc[...] = dk * LN2

    def key_step(i, gain):
        by_keys(i, key_block)
        kb = turns(i)
        dkv_buf[0, pl.ds(2 * kb, 2)] = dq_acc[...].astype(BF16).reshape(2, TOK, HD)

        @pl.when(core == 1)
        def _():
            swap(0, 2 * kb).start()
            swap(0, 2 * kb + 1).start()

        for half in range(2):
            block = 2 * kb + half
            rows = dq_acc[half * TOK:(half + 1) * TOK, :]
            both = turn_back(rows, cos_all[block], sin_all[block]) * k_unit[block]
            gain = gain + jnp.sum(both.reshape(TOK // 8, 8, HD), axis=0)

        @pl.when((core == 0) & (i > 0))
        def _():
            before = turns(i - 1)
            settle(0, 2 * before)
            settle(0, 2 * before + 1)

        return gain

    gain_k = lax.fori_loop(0, NBLK, key_step, jnp.zeros((8, HD), F32))
    row = lax.broadcasted_iota(jnp.int32, (8, HD), 0)
    gain_one[0] = jnp.where(
        row == 0,
        jnp.sum(gain_acc[...], axis=0, keepdims=True),
        jnp.where(row == 1, jnp.sum(gain_k, axis=0, keepdims=True), 0.0),
    )

    def share(stage, i):
        return pltpu.make_async_remote_copy(
            src_ref=gain_one.at[stage], dst_ref=stages.at[stage, rank[stage]],
            send_sem=stage_send, recv_sem=stage_recv.at[stage],
            device_id=member(stage, i), device_id_type=MESH,
        )

    def share_all(stage):
        def one(i, carry):
            @pl.when(i != rank[stage])
            def _():
                share(stage, i).start()

            return carry

        lax.fori_loop(0, 8, one, 0)
        stages[stage, rank[stage]] = gain_one[stage]

    def gathered(stage):
        wait_on(stages.at[stage, pl.ds(0, 7)], stage_recv.at[stage])
        return jnp.sum(stages[stage], axis=0)

    share_all(0)

    @pl.when(core == 0)
    def _():
        settle(0, 2 * turns(NBLK - 1))
        settle(0, 2 * turns(NBLK - 1) + 1)

    gain_one[1] = gathered(0)
    share_all(1)
    gain_one[2] = gathered(1)
    share_all(2)
    wait_on(kv_all.at[0], pass_send)
    wait_on(mate, swap_send)
    wait_on(stages.at[pl.ds(0, 3), pl.ds(0, 7)], stage_send)
    near_one = span == core

    @pl.when(near_one)
    def _():
        few = pl.ds(0, SEQ - 1)
        wait_on(g_buf.at[few], send_sem.at[0])
        wait_on(q_buf.at[few], send_sem.at[2])
        wait_on(seg_all.at[few], send_sem.at[3])
        wait_on(g_buf.at[few], send_sem.at[1])
        wait_on(dq_buf.at[few], back_send.at[0])
        wait_on(mine.at[few], back_send.at[1])

    @pl.when(jnp.logical_not(near_one))
    def _():
        wait_on(g_buf, send_sem.at[0])
        wait_on(q_buf, send_sem.at[2])
        wait_on(seg_all, send_sem.at[3])
        wait_on(g_buf, send_sem.at[1])
        wait_on(dq_buf, back_send.at[0])
        wait_on(mine, back_send.at[1])

    wait_on(dq_out, back_recv.at[0])
    wait_on(dkv_out, back_recv.at[1])
    total = gathered(2)
    gain_out[...] = jnp.where(
        row == 0, total / (qg_ref[...] * QMUL), total / kg_ref[...]
    )


def norm_kernel(
    where_ref, dq_ref, dkv_ref, q_ref, k_ref, qg_ref, kg_ref, gain_ref, near_ref, far_ref,
    gq_ref, gk_ref, gv_ref, gqg_ref, gkg_ref,
    q_wide, k_wide, q_new, k_new, v_new,
):
    cosine, sine = block_rope(near_ref, far_ref, where_ref[0])
    q_wide[...] = q_ref[...].astype(F32).reshape(TOK * 16, HD)
    k_wide[...] = k_ref[...].astype(F32).reshape(TOK * 8, HD)

    def back(wide, new, rows_at, upstream, gain):
        rows = wide[rows_at, :]
        size = lax.rsqrt(jnp.mean(rows * rows, axis=1, keepdims=True) + EPS)
        unit = rows * size
        slope = turn_back(upstream.astype(F32), cosine, sine) * gain
        new[rows_at, :] = size * (slope - unit * jnp.mean(slope * unit, axis=1, keepdims=True))

    for h in range(16):
        back(q_wide, q_new, pl.ds(h, TOK, stride=16), dq_ref[h], qg_ref[...])
    for j in range(8):
        back(k_wide, k_new, pl.ds(j, TOK, stride=8), dkv_ref[j], kg_ref[...])
        v_new[pl.ds(j, TOK, stride=8), :] = dkv_ref[8 + j].astype(F32)
    gq_ref[...] = q_new[...].reshape(TOK, 16, HD).astype(BF16)
    gk_ref[...] = k_new[...].reshape(TOK, 8, HD).astype(BF16)
    gv_ref[...] = v_new[...].reshape(TOK, 8, HD).astype(BF16)
    gqg_ref[...] = gain_ref[0:1, :]
    gkg_ref[...] = gain_ref[1:2, :]


def shape(dims, dtype):
    return jax.ShapeDtypeStruct(dims, dtype)


def body(q_pre, k_pre, values, grad_out, segment_ids, q_gain, k_gain):
    near, far = (jnp.asarray(table) for table in rope_tables())
    qg, kg = q_gain.reshape(1, HD), k_gain.reshape(1, HD)
    dma = pltpu.SemaphoreType.DMA
    tiles = (SEQ, TOK, HD)
    dq_back, dkv_back, gain_sums = pl.pallas_call(
        fused_kernel,
        name="heads_and_back",
        out_shape=(shape(tiles, BF16), shape(tiles, BF16), shape((8, HD), F32)),
        in_specs=[HBM] * 9,
        out_specs=(ANY, ANY, VM),
        scratch_shapes=[
            pltpu.VMEM((TOK, 16, HD), BF16), pltpu.VMEM((TOK, 8, HD), BF16),
            pltpu.VMEM((TOK, 8, HD), BF16), pltpu.VMEM((TOK, 16, HD), BF16),
            pltpu.VMEM((1, TOK), jnp.int32), pltpu.VMEM((1, HD), F32), pltpu.VMEM((1, HD), F32),
            pltpu.VMEM((2, TOK, HD), F32), pltpu.VMEM((SEQ, 2, HD), F32),
            pltpu.VMEM((TOK * 16, HD), F32), pltpu.VMEM((TOK * 8, HD), F32),
            pltpu.VMEM((TOK * 8, HD), F32), pltpu.VMEM((TOK * 16, HD), F32),
            pltpu.VMEM(tiles, BF16), pltpu.VMEM(tiles, BF16),
            pltpu.VMEM((2, 8, TOK, HD), BF16),
            pltpu.VMEM(tiles, BF16), pltpu.VMEM(tiles, BF16), pltpu.VMEM((2,) + tiles, BF16),
            pltpu.VMEM((SEQ, 1, TOK), jnp.int32), pltpu.VMEM((SEQ, 1, TOK), jnp.int32),
            pltpu.VMEM(tiles, F32), pltpu.VMEM(tiles, F32),
            pltpu.VMEM(tiles, F32), pltpu.VMEM(tiles, F32),
            pltpu.VMEM((BAND, BLK, BLK), F32), pltpu.VMEM((NBLK, BAND, BLK, BLK), BF16),
            pltpu.VMEM((BAND, BLK, BLK), F32), pltpu.VMEM((BLK, HD), F32),
            pltpu.VMEM((8, HD), F32),
            pltpu.VMEM(tiles, BF16), pltpu.VMEM((2,) + tiles, BF16),
            pltpu.VMEM(tiles, BF16), pltpu.VMEM(tiles, BF16),
            pltpu.VMEM((3, 8, HD), F32), pltpu.VMEM((3, 8, 8, HD), F32),
            dma((9,)), dma((4,)), dma((4,)), dma, dma, dma((SEQ,)),
            dma((2,)), dma((2,)), dma, dma((SEQ,)), dma, dma((3,)),
        ],
        compiler_params=pltpu.CompilerParams(
            collective_id=0, has_side_effects=True, vmem_limit_bytes=48 << 20
        ),
    )(*(
        pltpu.with_memory_space_constraint(x, pltpu.HBM)
        for x in (
            q_pre[0], k_pre[0], values[0], grad_out[0], segment_ids, qg, kg, near, far
        )
    ))

    where = lax.axis_index("seq").astype(jnp.int32).reshape(1)
    grad_q, grad_k, grad_v, grad_qg, grad_kg = pl.pallas_call(
        norm_kernel,
        name="norm_back",
        out_shape=(
            shape((TOK, 16, HD), BF16), shape((TOK, 8, HD), BF16), shape((TOK, 8, HD), BF16),
            shape((1, HD), F32), shape((1, HD), F32),
        ),
        in_specs=[pl.BlockSpec(memory_space=pltpu.SMEM)] + [VM] * 9,
        out_specs=(VM,) * 5,
        scratch_shapes=[
            pltpu.VMEM((TOK * 16, HD), F32), pltpu.VMEM((TOK * 8, HD), F32),
            pltpu.VMEM((TOK * 16, HD), F32), pltpu.VMEM((TOK * 8, HD), F32),
            pltpu.VMEM((TOK * 8, HD), F32),
        ],
        compiler_params=pltpu.CompilerParams(vmem_limit_bytes=32 << 20),
    )(where, dq_back, dkv_back, q_pre[0], k_pre[0], qg, kg, gain_sums, near, far)
    return (
        grad_q[None], grad_k[None], grad_v[None], grad_qg.reshape(HD), grad_kg.reshape(HD)
    )


def solution(mesh):
    tokens = P("dp", "seq", None, None)
    return jax.shard_map(
        body,
        mesh=mesh,
        in_specs=(tokens, tokens, tokens, tokens, P("dp", "seq"), P(), P()),
        out_specs=(tokens, tokens, tokens, P(), P()),
        check_vma=False,
    )
```

time: 78.6 us -> 71.6 us (0.911)
  local copies, waits for them, and re-layouts: 5.57 us -> 0.64 us
  Pallas kernels: 71.9 us -> 70.1 us
    unnamed x18 -> x12, local copies, waits for them, and re-layouts: 5.57 us -> 0.64 us
    pallas_call x1, Pallas kernels: 67.7 us -> 65.9 us  [body(): pl.pallas_call(fused_kernel, name='heads_and_back', out_shape=(shape(tile...]
where the time goes in v3:
time: 71.6 us; the launch traced here: 71.5 us
  Pallas kernels  70.1 us (98%)
  between operations  0.72 us (1%)
    pallas_call x1, Pallas kernels, body(): pl.pallas_call(fused_kernel, name='heads_and_back', out_shape=(shape(tile...  65.9 us
    pallas_call x1, Pallas kernels, body(): pl.pallas_call(norm_kernel, name='norm_back', out_shape=(shape((TOK, 16,...  4.2 us

profile of v3, /device:TPU:1, one launch (start us, length us, event | category | flops | bytes accessed | tf_op | source)
XLA Modules:
  0.0 71.5 jit_solution(5946259034923638095)
XLA Ops:
  0.6 0.0 copy-start
  0.6 0.0 copy-start.1
  0.7 0.0 copy-start.2
  0.7 0.0 copy-start.3
  0.7 65.9 %heads_and_back.1 = (bf16[16,128,128]{2,1,0:T(8,128)(2,1)S(1)}, bf16[16,128,128]{2,1,0:T(8,128)(2,1)S(1)}, f32[8,128]{1,0:T(8,128)S(1)}) custom-call(bf16[128,16,128]{2,1,0:T(8,128)(2,1)} %bitcast.12, bf16[128,8,128]{2,1,0:T(8,128)(2,1)} %bitcast.14, bf16[128,8,128]{2,1,0:T(8,128)(2,1)} %bitcast.21, bf16[128,16,128]{2,1,0:T(8,128)(2,1)} %bitcast.20, ...), custom_call_target="tpu_custom_call" | custom-call | tf_op jit(solution)/shard_map/heads_and_back/pallas_call | solution.py:578
  66.6 0.0 copy-start.4
  66.6 0.0 copy-start.5
  66.6 0.0 copy-done
  66.6 0.0 copy-done.1
  66.6 0.0 copy-done.2
  66.7 0.0 copy-done.3
  66.7 0.6 copy-done.4
  67.3 0.0 copy-done.5
  67.3 4.2 %norm_back.1 = (bf16[128,16,128]{2,1,0:T(8,128)(2,1)}, bf16[128,8,128]{2,1,0:T(8,128)(2,1)}, bf16[128,8,128]{2,1,0:T(8,128)(2,1)}, f32[1,128]{1,0:T(1,128)}, f32[1,128]{1,0:T(1,128)}) custom-call(s32[1]{0:T(128)} %bitcast.where_ref, bf16[16,128,128]{2,1,0:T(8,128)(2,1)S(1)} %get-tuple-element.13.dq_ref, bf16[16,128,128]{2,1,0:T(8,128)(2,1)S(1)} %get-tuple-element.14.dkv_ref, ...), custom_call_target="tpu_custom_call" | custom-call | tf_op jit(solution)/shard_map/norm_back/pallas_call | solution.py:617
Async XLA Ops:
  0.6 66.0 %copy-start = (bf16[1,128,16,128]{3,2,1,0:T(8,128)(2,1)S(1)}, bf16[1,128,16,128]{3,2,1,0:T(8,128)(2,1)}, u32[]{:S(2)}) copy-start(bf16[1,128,16,128]{3,2,1,0:T(8,128)(2,1)} %param.9) | copy-start | bytes 1572868
  0.6 66.0 %copy-start.1 = (bf16[1,128,8,128]{3,2,1,0:T(8,128)(2,1)S(1)}, bf16[1,128,8,128]{3,2,1,0:T(8,128)(2,1)}, u32[]{:S(2)}) copy-start(bf16[1,128,8,128]{3,2,1,0:T(8,128)(2,1)} %param.10) | copy-start | bytes 786436
  0.7 66.0 %copy-start.2 = (f32[2,128,128]{2,1,0:T(8,128)S(1)}, f32[2,128,128]{2,1,0:T(8,128)}, u32[]{:S(2)}) copy-start(f32[2,128,128]{2,1,0:T(8,128)} %constant.8.clone.near_hbm.near_ref) | copy-start | bytes 393220
  0.7 66.0 %copy-start.3 = (f32[16,2,128]{2,1,0:T(2,128)S(1)}, f32[16,2,128]{2,1,0:T(2,128)}, u32[]{:S(2)}) copy-start(f32[16,2,128]{2,1,0:T(2,128)} %constant.9.clone.far_hbm.far_ref) | copy-start | bytes 49156
  66.6 0.7 copy-start.4
  66.6 0.7 copy-start.5

commit v4 on v3

--- a/solution.py
+++ b/solution.py
@@ -25,7 +25,6 @@
 BF16 = jnp.bfloat16
 ANY = pl.BlockSpec(memory_space=pl.ANY)
 HBM = pl.BlockSpec(memory_space=pltpu.HBM)
-VM = pl.BlockSpec(memory_space=pltpu.VMEM)
 
 
 def rope_tables():
@@ -66,12 +65,12 @@
 
 def fused_kernel(
     q_hbm, k_hbm, v_hbm, g_hbm, seg_hbm, qg_hbm, kg_hbm, near_hbm, far_hbm,
-    dq_out, dkv_out, gain_out,
+    gq_out, gk_out, gv_out, gqg_out, gkg_out,
     q_raw, k_raw, v_raw, g_raw, seg_one, qg_ref, kg_ref, near_ref, far_ref,
-    q_wide, k_wide, v_wide, g_wide, q_buf, g_buf, kv_buf,
+    q_wide, k_wide, v_wide, g_wide, q_row, k_row, q_size, k_size, q_buf, g_buf, kv_buf,
     q_all, g_all, kv_all, seg_all, first_ref, cos_all, sin_all, q_unit, k_unit,
-    expo, prob, pgrad, dq_acc, gain_acc,
-    dq_buf, dkv_buf, mate, mine, gain_one, stages,
+    expo, prob, sgrad, pgrad, dq_acc, gain_acc,
+    dq_buf, dkv_buf, mate, mine, dq_out, dkv_out, gain_one, stages,
     load_sem, send_sem, recv_sem, pass_send, pass_recv, pass_got,
     back_send, back_recv, swap_send, swap_recv, stage_send, stage_recv,
 ):
@@ -103,39 +102,41 @@
 
         return carry
 
-    x_at, y_at = lax.rem(s, 4), lax.div(s, 4)
-    z_low, z_high = lax.rem(z, 2), lax.div(z, 2)
+    sizes = (16, 32)
+    rank = (z, core * SEQ + s)
 
     def member(stage, i):
         if stage == 0:
-            return (2 * z + lax.rem(i, 2), 4 * y_at + lax.div(i, 2))
-        if stage == 1:
-            return (2 * (2 * z_high + lax.rem(i, 2)) + core, 4 * lax.div(i, 2) + x_at)
-        return (2 * (2 * i + z_low) + core, s)
-
-    rank = (2 * x_at + core, 2 * y_at + z_low, z_high)
-
-    def greet_low(i, carry):
-        pl.semaphore_signal(
-            barrier, inc=1, device_id=member(1, 2 * i + 1 - z_low), device_id_type=MESH
-        )
-        return carry
-
-    def greet_high(i, carry):
-        @pl.when(i != z_high)
-        def _():
-            pl.semaphore_signal(barrier, inc=1, device_id=member(2, i), device_id_type=MESH)
+            return (2 * i + core, s)
+        return (2 * z + lax.div(i, SEQ), lax.rem(i, SEQ))
+
+    def greet_z(i, carry):
+        @pl.when(i != z)
+        def _():
+            pl.semaphore_signal(barrier, inc=1, device_id=member(0, i), device_id_type=MESH)
 
         return carry
 
     lax.fori_loop(0, 2 * SEQ, greet, 0)
-    lax.fori_loop(0, 4, greet_low, 0)
-    lax.fori_loop(0, 8, greet_high, 0)
+    lax.fori_loop(0, 16, greet_z, 0)
     for copy in loads[:6]:
         copy.wait()
     cosine, sine = block_rope(near_ref, far_ref, s)
     k_wide[...] = k_raw[...].astype(F32).reshape(TOK * 8, HD)
-    pl.semaphore_wait(barrier, 2 * SEQ - 1 + 4 + 7)
+
+    def prepare(wide, rows_at, gain, row, size_at):
+        rows = wide[rows_at, :]
+        size = lax.rsqrt(jnp.mean(rows * rows, axis=1, keepdims=True) + EPS)
+        unit = rows * size
+        row[...] = unit
+        size_at[...] = jnp.broadcast_to(size, (TOK, HD))
+        return turn(unit * gain, cosine, sine)
+
+    for j in range(8):
+        kv_buf[0, j] = prepare(
+            k_wide, pl.ds(j, TOK, stride=8), kg_ref[...], k_row.at[j], k_size.at[j]
+        ).astype(BF16)
+    pl.semaphore_wait(barrier, 2 * SEQ - 1 + 15)
 
     def is_me(j, r):
         return (2 * z + r == dp) & (2 * j + core == s)
@@ -176,12 +177,7 @@
 
     def send_k(t, carry):
         j = turns(t)
-        rows = k_wide[pl.ds(j, TOK, stride=8), :]
-        size = lax.rsqrt(jnp.mean(rows * rows, axis=1, keepdims=True) + EPS)
-        kv_buf[0, j] = turn(rows * size * kg_ref[...], cosine, sine).astype(BF16)
         send(part_of(1, j, 0), j, 0)
-        for r in range(2):
-            send(part_of(3, j, r), j, r)
         return carry
 
     lax.fori_loop(0, 8, send_k, 0)
@@ -192,13 +188,31 @@
         j = turns(t)
         for r in range(2):
             h = 2 * j + r
-            rows = q_wide[pl.ds(h, TOK, stride=16), :]
-            size = lax.rsqrt(jnp.mean(rows * rows, axis=1, keepdims=True) + EPS)
-            q_buf[h] = (turn(rows * size * qg_ref[...], cosine, sine) * QMUL).astype(BF16)
+            q_buf[h] = (prepare(
+                q_wide, pl.ds(h, TOK, stride=16), qg_ref[...], q_row.at[h], q_size.at[h]
+            ) * QMUL).astype(BF16)
             send(part_of(2, j, r), j, r)
         return carry
 
     lax.fori_loop(0, 8, send_q, 0)
+
+    def send_seg(t, carry):
+        j = turns(t)
+        for r in range(2):
+            send(part_of(3, j, r), j, r)
+        return carry
+
+    lax.fori_loop(0, 8, send_seg, 0)
+    loads[7].wait()
+    v_wide[...] = v_raw[...].astype(F32).reshape(TOK * 8, HD)
+
+    def send_v(t, carry):
+        j = turns(t)
+        kv_buf[1, j] = v_wide[pl.ds(j, TOK, stride=8), :].astype(BF16)
+        send(part_of(1, j, 1), j, 1)
+        return carry
+
+    lax.fori_loop(0, 8, send_v, 0)
     loads[8].wait()
     g_wide[...] = g_raw[...].astype(F32).reshape(TOK * 16, HD)
 
@@ -212,16 +226,6 @@
 
     lax.fori_loop(0, 8, send_g, 0)
 
-    loads[7].wait()
-    v_wide[...] = v_raw[...].astype(F32).reshape(TOK * 8, HD)
-
-    def send_v(t, carry):
-        j = turns(t)
-        kv_buf[1, j] = v_wide[pl.ds(j, TOK, stride=8), :].astype(BF16)
-        send(part_of(1, j, 1), j, 1)
-        return carry
-
-    lax.fori_loop(0, 8, send_v, 0)
     def passing(kind, t):
         return pltpu.make_async_remote_copy(
             src_ref=kv_all.at[kind, t], dst_ref=kv_all.at[kind, t],
@@ -233,7 +237,7 @@
         pltpu.make_async_copy(ref, ref, sem).wait()
 
     def forward(i, carry):
-        t = lax.rem(s + i, SEQ)
+        t = lax.rem(2 * (j_own + SEQ // 2 - lax.div(i, 2)) + lax.rem(i, 2), SEQ)
         wait_on(kv_all.at[core, t], pass_got.at[t])
         passing(core, t).start()
         return carry
@@ -315,6 +319,12 @@
 
     def forward_step(i, carry):
         by_queries(i, forward_block)
+
+        @pl.when(core == 1)
+        def _():
+            forward(2 * i, 0)
+            forward(2 * i + 1, 0)
+
         return carry
 
     lax.fori_loop(0, NBLK, forward_step, 0)
@@ -327,6 +337,10 @@
 
     lax.fori_loop(0, SEQ, units, 0)
     wait_on(g_all, recv_sem.at[0])
+
+    @pl.when(core == 0)
+    def _():
+        wait_on(kv_all.at[1], pass_recv)
 
     def swap(kind, t):
         return pltpu.make_async_remote_copy(
@@ -335,34 +349,6 @@
             device_id=mate_at, device_id_type=MESH,
         )
 
-    def value_block(kb, count):
-        dv = jnp.dot(prob[kb, 0], pair(g_all, kb), preferred_element_type=F32)
-        for d in range(1, count):
-            dv = dv + jnp.dot(prob[kb + d, d], pair(g_all, kb + d), preferred_element_type=F32)
-        dkv_buf[1, pl.ds(2 * kb, 2)] = dv.astype(BF16).reshape(2, TOK, HD)
-
-    def value_step(i, carry):
-        by_keys(i, value_block)
-        kb = turns(i)
-
-        @pl.when(core == 0)
-        def _():
-            swap(1, 2 * kb).start()
-            swap(1, 2 * kb + 1).start()
-
-        @pl.when(core == 1)
-        def _():
-            forward(2 * i, 0)
-            forward(2 * i + 1, 0)
-
-        return carry
-
-    lax.fori_loop(0, NBLK, value_step, 0)
-
-    @pl.when(core == 0)
-    def _():
-        wait_on(kv_all.at[1], pass_recv)
-
     slot_q = 2 * j_own + core
     slot_kv = core * 8 + j_own
 
@@ -395,6 +381,10 @@
         swap(kind, t).wait_recv()
         mine[t] = (dkv_buf[kind, t].astype(F32) + mate[t].astype(F32)).astype(BF16)
         send_back(back_part(1, t), t)
+
+    def settle_pair(kind, i):
+        settle(kind, 2 * turns(i))
+        settle(kind, 2 * turns(i) + 1)
 
     def backward_block(qi, count):
         upstream = pair(g_all, qi)
@@ -409,7 +399,7 @@
         dq = jnp.zeros((BLK, HD), F32)
         for d in range(count):
             ds = (prob[qi, d].astype(F32) * (pgrad[d] - delta)).astype(BF16)
-            prob[qi, d] = ds
+            sgrad[qi, d] = ds
             dq = dq + lax.dot_general(ds, keys_of(0, qi - d), lead, preferred_element_type=F32)
         dq_acc[...] = dq * SCALE
 
@@ -426,19 +416,14 @@
             gain = gain + jnp.sum(both.reshape(TOK // 8, 8, HD), axis=0)
         gain_acc[...] = gain
 
-        @pl.when(core == 1)
-        def _():
-            settle(1, 2 * qi)
-            settle(1, 2 * qi + 1)
-
         return carry
 
     lax.fori_loop(0, NBLK, backward_step, 0)
 
     def key_block(kb, count):
-        dk = jnp.dot(prob[kb, 0], pair(q_all, kb), preferred_element_type=F32)
+        dk = jnp.dot(sgrad[kb, 0], pair(q_all, kb), preferred_element_type=F32)
         for d in range(1, count):
-            dk = dk + jnp.dot(prob[kb + d, d], pair(q_all, kb + d), preferred_element_type=F32)
+            dk = dk + jnp.dot(sgrad[kb + d, d], pair(q_all, kb + d), preferred_element_type=F32)
         dq_acc[...] = dk * LN2
 
     def key_step(i, gain):
@@ -459,9 +444,7 @@
 
         @pl.when((core == 0) & (i > 0))
         def _():
-            before = turns(i - 1)
-            settle(0, 2 * before)
-            settle(0, 2 * before + 1)
+            settle_pair(0, i - 1)
 
         return gain
 
@@ -476,7 +459,7 @@
     def share(stage, i):
         return pltpu.make_async_remote_copy(
             src_ref=gain_one.at[stage], dst_ref=stages.at[stage, rank[stage]],
-            send_sem=stage_send, recv_sem=stage_recv.at[stage],
+            send_sem=stage_send.at[stage], recv_sem=stage_recv.at[stage],
             device_id=member(stage, i), device_id_type=MESH,
         )
 
@@ -488,27 +471,71 @@
 
             return carry
 
-        lax.fori_loop(0, 8, one, 0)
+        lax.fori_loop(0, sizes[stage], one, 0)
         stages[stage, rank[stage]] = gain_one[stage]
 
     def gathered(stage):
-        wait_on(stages.at[stage, pl.ds(0, 7)], stage_recv.at[stage])
-        return jnp.sum(stages[stage], axis=0)
+        wait_on(stages.at[stage, pl.ds(0, sizes[stage] - 1)], stage_recv.at[stage])
+        return jnp.sum(stages[stage, 0:sizes[stage]], axis=0)
 
     share_all(0)
 
     @pl.when(core == 0)
     def _():
-        settle(0, 2 * turns(NBLK - 1))
-        settle(0, 2 * turns(NBLK - 1) + 1)
+        settle_pair(0, NBLK - 1)
+
+    def value_block(kb, count):
+        dv = jnp.dot(prob[kb, 0], pair(g_all, kb), preferred_element_type=F32)
+        for d in range(1, count):
+            dv = dv + jnp.dot(prob[kb + d, d], pair(g_all, kb + d), preferred_element_type=F32)
+        dkv_buf[1, pl.ds(2 * kb, 2)] = dv.astype(BF16).reshape(2, TOK, HD)
+
+    def value_step(i, carry):
+        by_keys(i, value_block)
+        kb = turns(i)
+
+        @pl.when(core == 0)
+        def _():
+            swap(1, 2 * kb).start()
+            swap(1, 2 * kb + 1).start()
+
+        @pl.when((core == 1) & (i > 0))
+        def _():
+            settle_pair(1, i - 1)
+
+        return carry
+
+    lax.fori_loop(0, NBLK, value_step, 0)
+
+    @pl.when(core == 1)
+    def _():
+        settle_pair(1, NBLK - 1)
 
     gain_one[1] = gathered(0)
     share_all(1)
-    gain_one[2] = gathered(1)
-    share_all(2)
+
+    def norm_back(upstream, gain, unit, size):
+        slope = turn_back(upstream.astype(F32), cosine, sine) * gain
+        return size * (slope - unit * jnp.mean(slope * unit, axis=1, keepdims=True))
+
+    wait_on(dq_out, back_recv.at[0])
+    for h in range(16):
+        q_wide[pl.ds(h, TOK, stride=16), :] = norm_back(
+            dq_out[h], qg_ref[...], q_row[h], q_size[h]
+        )
+    gq_out[...] = q_wide[...].reshape(TOK, 16, HD).astype(BF16)
+    wait_on(dkv_out, back_recv.at[1])
+    for j in range(8):
+        k_wide[pl.ds(j, TOK, stride=8), :] = norm_back(
+            dkv_out[j], kg_ref[...], k_row[j], k_size[j]
+        )
+    gk_out[...] = k_wide[...].reshape(TOK, 8, HD).astype(BF16)
+    for j in range(8):
+        v_wide[pl.ds(j, TOK, stride=8), :] = dkv_out[8 + j].astype(F32)
+    gv_out[...] = v_wide[...].reshape(TOK, 8, HD).astype(BF16)
     wait_on(kv_all.at[0], pass_send)
     wait_on(mate, swap_send)
-    wait_on(stages.at[pl.ds(0, 3), pl.ds(0, 7)], stage_send)
+    wait_on(stages.at[0, pl.ds(0, 15)], stage_send.at[0])
     near_one = span == core
 
     @pl.when(near_one)
@@ -530,40 +557,10 @@
         wait_on(dq_buf, back_send.at[0])
         wait_on(mine, back_send.at[1])
 
-    wait_on(dq_out, back_recv.at[0])
-    wait_on(dkv_out, back_recv.at[1])
-    total = gathered(2)
-    gain_out[...] = jnp.where(
-        row == 0, total / (qg_ref[...] * QMUL), total / kg_ref[...]
-    )
-
-
-def norm_kernel(
-    where_ref, dq_ref, dkv_ref, q_ref, k_ref, qg_ref, kg_ref, gain_ref, near_ref, far_ref,
-    gq_ref, gk_ref, gv_ref, gqg_ref, gkg_ref,
-    q_wide, k_wide, q_new, k_new, v_new,
-):
-    cosine, sine = block_rope(near_ref, far_ref, where_ref[0])
-    q_wide[...] = q_ref[...].astype(F32).reshape(TOK * 16, HD)
-    k_wide[...] = k_ref[...].astype(F32).reshape(TOK * 8, HD)
-
-    def back(wide, new, rows_at, upstream, gain):
-        rows = wide[rows_at, :]
-        size = lax.rsqrt(jnp.mean(rows * rows, axis=1, keepdims=True) + EPS)
-        unit = rows * size
-        slope = turn_back(upstream.astype(F32), cosine, sine) * gain
-        new[rows_at, :] = size * (slope - unit * jnp.mean(slope * unit, axis=1, keepdims=True))
-
-    for h in range(16):
-        back(q_wide, q_new, pl.ds(h, TOK, stride=16), dq_ref[h], qg_ref[...])
-    for j in range(8):
-        back(k_wide, k_new, pl.ds(j, TOK, stride=8), dkv_ref[j], kg_ref[...])
-        v_new[pl.ds(j, TOK, stride=8), :] = dkv_ref[8 + j].astype(F32)
-    gq_ref[...] = q_new[...].reshape(TOK, 16, HD).astype(BF16)
-    gk_ref[...] = k_new[...].reshape(TOK, 8, HD).astype(BF16)
-    gv_ref[...] = v_new[...].reshape(TOK, 8, HD).astype(BF16)
-    gqg_ref[...] = gain_ref[0:1, :]
-    gkg_ref[...] = gain_ref[1:2, :]
+    wait_on(stages.at[1, pl.ds(0, 31)], stage_send.at[1])
+    total = gathered(1)
+    gqg_out[...] = total[0:1, :] / (qg_ref[...] * QMUL)
+    gkg_out[...] = total[1:2, :] / kg_ref[...]
 
 
 def shape(dims, dtype):
@@ -575,12 +572,16 @@
     qg, kg = q_gain.reshape(1, HD), k_gain.reshape(1, HD)
     dma = pltpu.SemaphoreType.DMA
     tiles = (SEQ, TOK, HD)
-    dq_back, dkv_back, gain_sums = pl.pallas_call(
+    kinds = (
+        shape((TOK, 16, HD), BF16), shape((TOK, 8, HD), BF16), shape((TOK, 8, HD), BF16),
+        shape((1, HD), F32), shape((1, HD), F32),
+    )
+    grad_q, grad_k, grad_v, grad_qg, grad_kg = pl.pallas_call(
         fused_kernel,
         name="heads_and_back",
-        out_shape=(shape(tiles, BF16), shape(tiles, BF16), shape((8, HD), F32)),
+        out_shape=kinds,
         in_specs=[HBM] * 9,
-        out_specs=(ANY, ANY, VM),
+        out_specs=(pl.BlockSpec(memory_space=pltpu.VMEM),) * 5,
         scratch_shapes=[
             pltpu.VMEM((TOK, 16, HD), BF16), pltpu.VMEM((TOK, 8, HD), BF16),
             pltpu.VMEM((TOK, 8, HD), BF16), pltpu.VMEM((TOK, 16, HD), BF16),
@@ -588,6 +589,8 @@
             pltpu.VMEM((2, TOK, HD), F32), pltpu.VMEM((SEQ, 2, HD), F32),
             pltpu.VMEM((TOK * 16, HD), F32), pltpu.VMEM((TOK * 8, HD), F32),
             pltpu.VMEM((TOK * 8, HD), F32), pltpu.VMEM((TOK * 16, HD), F32),
+            pltpu.VMEM(tiles, F32), pltpu.VMEM((8, TOK, HD), F32),
+            pltpu.VMEM(tiles, F32), pltpu.VMEM((8, TOK, HD), F32),
             pltpu.VMEM(tiles, BF16), pltpu.VMEM(tiles, BF16),
             pltpu.VMEM((2, 8, TOK, HD), BF16),
             pltpu.VMEM(tiles, BF16), pltpu.VMEM(tiles, BF16), pltpu.VMEM((2,) + tiles, BF16),
@@ -595,13 +598,15 @@
             pltpu.VMEM(tiles, F32), pltpu.VMEM(tiles, F32),
             pltpu.VMEM(tiles, F32), pltpu.VMEM(tiles, F32),
             pltpu.VMEM((BAND, BLK, BLK), F32), pltpu.VMEM((NBLK, BAND, BLK, BLK), BF16),
+            pltpu.VMEM((NBLK, BAND, BLK, BLK), BF16),
             pltpu.VMEM((BAND, BLK, BLK), F32), pltpu.VMEM((BLK, HD), F32),
             pltpu.VMEM((8, HD), F32),
             pltpu.VMEM(tiles, BF16), pltpu.VMEM((2,) + tiles, BF16),
             pltpu.VMEM(tiles, BF16), pltpu.VMEM(tiles, BF16),
-            pltpu.VMEM((3, 8, HD), F32), pltpu.VMEM((3, 8, 8, HD), F32),
+            pltpu.VMEM(tiles, BF16), pltpu.VMEM(tiles, BF16),
+            pltpu.VMEM((2, 8, HD), F32), pltpu.VMEM((2, 32, 8, HD), F32),
             dma((9,)), dma((4,)), dma((4,)), dma, dma, dma((SEQ,)),
-            dma((2,)), dma((2,)), dma, dma((SEQ,)), dma, dma((3,)),
+            dma((2,)), dma((2,)), dma, dma((SEQ,)), dma((2,)), dma((2,)),
         ],
         compiler_params=pltpu.CompilerParams(
             collective_id=0, has_side_effects=True, vmem_limit_bytes=48 << 20
@@ -613,23 +618,6 @@
         )
     ))
 
-    where = lax.axis_index("seq").astype(jnp.int32).reshape(1)
-    grad_q, grad_k, grad_v, grad_qg, grad_kg = pl.pallas_call(
-        norm_kernel,
-        name="norm_back",
-        out_shape=(
-            shape((TOK, 16, HD), BF16), shape((TOK, 8, HD), BF16), shape((TOK, 8, HD), BF16),
-            shape((1, HD), F32), shape((1, HD), F32),
-        ),
-        in_specs=[pl.BlockSpec(memory_space=pltpu.SMEM)] + [VM] * 9,
-        out_specs=(VM,) * 5,
-        scratch_shapes=[
-            pltpu.VMEM((TOK * 16, HD), F32), pltpu.VMEM((TOK * 8, HD), F32),
-            pltpu.VMEM((TOK * 16, HD), F32), pltpu.VMEM((TOK * 8, HD), F32),
-            pltpu.VMEM((TOK * 8, HD), F32),
-        ],
-        compiler_params=pltpu.CompilerParams(vmem_limit_bytes=32 << 20),
-    )(where, dq_back, dkv_back, q_pre[0], k_pre[0], qg, kg, gain_sums, near, far)
     return (
         grad_q[None], grad_k[None], grad_v[None], grad_qg.reshape(HD), grad_kg.reshape(HD)
     )

time: 71.6 us -> 65.9 us (0.920)
  Pallas kernels: 70.1 us -> 61.9 us
  local copies, waits for them, and re-layouts: 0.64 us -> 3.22 us
    pallas_call x2 -> x1, Pallas kernels: 70.1 us -> 61.9 us  [body(): pl.pallas_call(fused_kernel, name='heads_and_back', out_shape=kinds, in_s...]
    unnamed x12 -> x5, local copies, waits for them, and re-layouts: 0.64 us -> 3.22 us
where the time goes in v4:
time: 65.9 us; the launch traced here: 65.7 us
  Pallas kernels  61.9 us (94%)
  local copies, waits for them, and re-layouts  3.22 us (5%)
    pallas_call x1, Pallas kernels, body(): pl.pallas_call(fused_kernel, name='heads_and_back', out_shape=kinds, in_s...  61.9 us
    unnamed x5, local copies, waits for them, and re-layouts  3.22 us

profile of v4, /device:TPU:1, one launch (start us, length us, event | category | flops | bytes accessed | tf_op | source)
XLA Modules:
  0.0 65.7 jit_solution(9937374023422587071)
XLA Ops:
  0.6 61.9 %heads_and_back.1 = (bf16[128,16,128]{2,1,0:T(8,128)(2,1)S(1)}, bf16[128,8,128]{2,1,0:T(8,128)(2,1)S(1)}, bf16[128,8,128]{2,1,0:T(8,128)(2,1)S(1)}, f32[1,128]{1,0:T(1,128)S(1)}, f32[1,128]{1,0:T(1,128)S(1)}) custom-call(bf16[128,16,128]{2,1,0:T(8,128)(2,1)} %bitcast.16, bf16[128,8,128]{2,1,0:T(8,128)(2,1)} %bitcast.18, bf16[128,8,128]{2,1,0:T(8,128)(2,1)} %bitcast.19, ...), custom_call_target="tpu_custom_call" | custom-call | tf_op jit(solution)/shard_map/heads_and_back/pallas_call | solution.py:579
  62.5 0.8 %copy.19 = bf16[1,128,16,128]{3,2,1,0:T(8,128)(2,1)} copy(bf16[1,128,16,128]{3,2,1,0:T(8,128)(2,1)S(1)} %bitcast.11) | data formatting | bytes 1048576
  63.3 0.7 %copy.20 = bf16[1,128,8,128]{3,2,1,0:T(8,128)(2,1)} copy(bf16[1,128,8,128]{3,2,1,0:T(8,128)(2,1)S(1)} %bitcast.13) | data formatting | bytes 524288
  64.0 0.7 %copy.21 = bf16[1,128,8,128]{3,2,1,0:T(8,128)(2,1)} copy(bf16[1,128,8,128]{3,2,1,0:T(8,128)(2,1)S(1)} %bitcast.12) | data formatting | bytes 524288
  64.7 0.5 copy.22
  65.2 0.5 copy.23

commit v5 on v4

--- a/solution.py
+++ b/solution.py
@@ -70,9 +70,9 @@
     q_wide, k_wide, v_wide, g_wide, q_row, k_row, q_size, k_size, q_buf, g_buf, kv_buf,
     q_all, g_all, kv_all, seg_all, first_ref, cos_all, sin_all, q_unit, k_unit,
     expo, prob, sgrad, pgrad, dq_acc, gain_acc,
-    dq_buf, dkv_buf, mate, mine, dq_out, dkv_out, gain_one, stages,
-    load_sem, send_sem, recv_sem, pass_send, pass_recv, pass_got,
-    back_send, back_recv, swap_send, swap_recv, stage_send, stage_recv,
+    dq_buf, dkv_buf, mate, mine, dq_out, dkv_out, gain_one, stages, gain_two,
+    load_sem, send_sem, recv_sem, pass_send, pass_recv, pass_got, g_got,
+    back_send, back_recv, swap_send, swap_recv, stage_send, stage_recv, store_sem,
 ):
     dp, s, z, core = place()
     j_own = lax.div(s, 2)
@@ -142,6 +142,8 @@
         return (2 * z + r == dp) & (2 * j + core == s)
 
     def landing(kind):
+        if kind == 0:
+            return g_got.at[s]
         return recv_sem.at[kind] if kind != 1 else pass_got.at[s]
 
     def outward(kind, src, dst, j, r):
@@ -281,8 +283,7 @@
     def fold(x):
         return jnp.sum(x.reshape(BLK // 8, 8, BLK), axis=0)
 
-    def by_queries(i, run):
-        qi = turns(i)
+    def by_queries(qi, run):
         for count in range(1, BAND + 1):
             fits = (qi >= BAND - 1) if count == BAND else (qi == count - 1)
 
@@ -318,7 +319,7 @@
             prob[qi, d] = (expo[d] * inv).astype(BF16)
 
     def forward_step(i, carry):
-        by_queries(i, forward_block)
+        by_queries(turns(i), forward_block)
 
         @pl.when(core == 1)
         def _():
@@ -336,7 +337,6 @@
         return carry
 
     lax.fori_loop(0, SEQ, units, 0)
-    wait_on(g_all, recv_sem.at[0])
 
     @pl.when(core == 0)
     def _():
@@ -404,8 +404,10 @@
         dq_acc[...] = dq * SCALE
 
     def backward_step(i, carry):
-        by_queries(i, backward_block)
-        qi = turns(i)
+        qi = lax.rem(j_own + NBLK - i, NBLK)
+        for half in range(2):
+            wait_on(g_all.at[2 * qi + half], g_got.at[2 * qi + half])
+        by_queries(qi, backward_block)
         gain = gain_acc[...]
         for half in range(2):
             block = 2 * qi + half
@@ -523,16 +525,28 @@
         q_wide[pl.ds(h, TOK, stride=16), :] = norm_back(
             dq_out[h], qg_ref[...], q_row[h], q_size[h]
         )
-    gq_out[...] = q_wide[...].reshape(TOK, 16, HD).astype(BF16)
+    q_raw[...] = q_wide[...].reshape(TOK, 16, HD).astype(BF16)
+    stores = [
+        pltpu.make_async_copy(src, dst, store_sem.at[i])
+        for i, (src, dst) in enumerate(
+            (
+                (q_raw, gq_out), (k_raw, gk_out), (v_raw, gv_out),
+                (gain_two.at[0], gqg_out), (gain_two.at[1], gkg_out),
+            )
+        )
+    ]
+    stores[0].start()
     wait_on(dkv_out, back_recv.at[1])
     for j in range(8):
         k_wide[pl.ds(j, TOK, stride=8), :] = norm_back(
             dkv_out[j], kg_ref[...], k_row[j], k_size[j]
         )
-    gk_out[...] = k_wide[...].reshape(TOK, 8, HD).astype(BF16)
+    k_raw[...] = k_wide[...].reshape(TOK, 8, HD).astype(BF16)
+    stores[1].start()
     for j in range(8):
         v_wide[pl.ds(j, TOK, stride=8), :] = dkv_out[8 + j].astype(F32)
-    gv_out[...] = v_wide[...].reshape(TOK, 8, HD).astype(BF16)
+    v_raw[...] = v_wide[...].reshape(TOK, 8, HD).astype(BF16)
+    stores[2].start()
     wait_on(kv_all.at[0], pass_send)
     wait_on(mate, swap_send)
     wait_on(stages.at[0, pl.ds(0, 15)], stage_send.at[0])
@@ -559,8 +573,20 @@
 
     wait_on(stages.at[1, pl.ds(0, 31)], stage_send.at[1])
     total = gathered(1)
-    gqg_out[...] = total[0:1, :] / (qg_ref[...] * QMUL)
-    gkg_out[...] = total[1:2, :] / kg_ref[...]
+    gain_two[0] = total[0:1, :] / (qg_ref[...] * QMUL)
+    gain_two[1] = total[1:2, :] / kg_ref[...]
+    stores[3].start()
+    stores[4].start()
+    for copy in stores:
+        copy.wait()
+
+
+def store_kernel(q_ref, k_ref, v_ref, qg_ref, kg_ref, q_to, k_to, v_to, qg_to, kg_to):
+    q_to[...] = q_ref[...]
+    k_to[...] = k_ref[...]
+    v_to[...] = v_ref[...]
+    qg_to[...] = qg_ref[...]
+    kg_to[...] = kg_ref[...]
 
 
 def shape(dims, dtype):
@@ -576,12 +602,12 @@
         shape((TOK, 16, HD), BF16), shape((TOK, 8, HD), BF16), shape((TOK, 8, HD), BF16),
         shape((1, HD), F32), shape((1, HD), F32),
     )
-    grad_q, grad_k, grad_v, grad_qg, grad_kg = pl.pallas_call(
+    results = pl.pallas_call(
         fused_kernel,
         name="heads_and_back",
         out_shape=kinds,
         in_specs=[HBM] * 9,
-        out_specs=(pl.BlockSpec(memory_space=pltpu.VMEM),) * 5,
+        out_specs=(ANY,) * 5,
         scratch_shapes=[
             pltpu.VMEM((TOK, 16, HD), BF16), pltpu.VMEM((TOK, 8, HD), BF16),
             pltpu.VMEM((TOK, 8, HD), BF16), pltpu.VMEM((TOK, 16, HD), BF16),
@@ -605,8 +631,9 @@
             pltpu.VMEM(tiles, BF16), pltpu.VMEM(tiles, BF16),
             pltpu.VMEM(tiles, BF16), pltpu.VMEM(tiles, BF16),
             pltpu.VMEM((2, 8, HD), F32), pltpu.VMEM((2, 32, 8, HD), F32),
-            dma((9,)), dma((4,)), dma((4,)), dma, dma, dma((SEQ,)),
-            dma((2,)), dma((2,)), dma, dma((SEQ,)), dma((2,)), dma((2,)),
+            pltpu.VMEM((2, 1, HD), F32),
+            dma((9,)), dma((4,)), dma((4,)), dma, dma, dma((SEQ,)), dma((SEQ,)),
+            dma((2,)), dma((2,)), dma, dma((SEQ,)), dma((2,)), dma((2,)), dma((5,)),
         ],
         compiler_params=pltpu.CompilerParams(
             collective_id=0, has_side_effects=True, vmem_limit_bytes=48 << 20
@@ -618,6 +645,14 @@
         )
     ))
 
+    grad_q, grad_k, grad_v, grad_qg, grad_kg = pl.pallas_call(
+        store_kernel,
+        name="store_results",
+        out_shape=kinds,
+        in_specs=[pl.BlockSpec(memory_space=pltpu.VMEM)] * 5,
+        out_specs=(pl.BlockSpec(memory_space=pltpu.VMEM),) * 5,
+        compiler_params=pltpu.CompilerParams(vmem_limit_bytes=32 << 20),
+    )(*results)
     return (
         grad_q[None], grad_k[None], grad_v[None], grad_qg.reshape(HD), grad_kg.reshape(HD)
     )

time: 65.9 us -> 61.2 us (0.929)
  local copies, waits for them, and re-layouts: 3.22 us -> 0 us
  Pallas kernels: 61.9 us -> 60.4 us
    unnamed x5 -> x0, local copies, waits for them, and re-layouts: 3.22 us -> none
    pallas_call x1, Pallas kernels: 61.9 us -> 59.3 us  [body(): pl.pallas_call(fused_kernel, name='heads_and_back', out_shape=kinds, in_s...]
    pallas_call x0 -> x1, Pallas kernels: none -> 1.04 us  [body(): pl.pallas_call(store_kernel, name='store_results', out_shape=kinds, in_sp...]
where the time goes in v5:
time: 61.2 us; the launch traced here: 61 us
  Pallas kernels  60.4 us (99%)
  between operations  0.64 us (1%)
    pallas_call x1, Pallas kernels, body(): pl.pallas_call(fused_kernel, name='heads_and_back', out_shape=kinds, in_s...  59.3 us

profile of v5, /device:TPU:1, one launch (start us, length us, event | category | flops | bytes accessed | tf_op | source)
XLA Modules:
  0.0 61.0 jit_solution(9461778038654387915)
XLA Ops:
  0.6 59.3 %heads_and_back.1 = (bf16[128,16,128]{2,1,0:T(8,128)(2,1)S(1)}, bf16[128,8,128]{2,1,0:T(8,128)(2,1)S(1)}, bf16[128,8,128]{2,1,0:T(8,128)(2,1)S(1)}, f32[1,128]{1,0:T(1,128)S(1)}, f32[1,128]{1,0:T(1,128)S(1)}) custom-call(bf16[128,16,128]{2,1,0:T(8,128)(2,1)} %bitcast.11, bf16[128,8,128]{2,1,0:T(8,128)(2,1)} %bitcast.13, bf16[128,8,128]{2,1,0:T(8,128)(2,1)} %bitcast.14, ...), custom_call_target="tpu_custom_call" | custom-call | tf_op jit(solution)/shard_map/heads_and_back/pallas_call | solution.py:605
  60.0 1.0 %store_results.1 = (bf16[128,16,128]{2,1,0:T(8,128)(2,1)}, bf16[128,8,128]{2,1,0:T(8,128)(2,1)}, bf16[128,8,128]{2,1,0:T(8,128)(2,1)}, f32[1,128]{1,0:T(1,128)}, f32[1,128]{1,0:T(1,128)}) custom-call(bf16[128,16,128]{2,1,0:T(8,128)(2,1)S(1)} %get-tuple-element.15.q_ref, bf16[128,8,128]{2,1,0:T(8,128)(2,1)S(1)} %get-tuple-element.16.k_ref, ...), custom_call_target="tpu_custom_call" | custom-call | tf_op jit(solution)/shard_map/store_results/pallas_call | solution.py:648

commit v6 on v5

--- a/solution.py
+++ b/solution.py
@@ -71,7 +71,7 @@
     q_all, g_all, kv_all, seg_all, first_ref, cos_all, sin_all, q_unit, k_unit,
     expo, prob, sgrad, pgrad, dq_acc, gain_acc,
     dq_buf, dkv_buf, mate, mine, dq_out, dkv_out, gain_one, stages, gain_two,
-    load_sem, send_sem, recv_sem, pass_send, pass_recv, pass_got, g_got,
+    load_sem, send_sem, recv_sem, pass_send, pass_recv, pass_got, g_got, q_got,
     back_send, back_recv, swap_send, swap_recv, stage_send, stage_recv, store_sem,
 ):
     dp, s, z, core = place()
@@ -144,6 +144,8 @@
     def landing(kind):
         if kind == 0:
             return g_got.at[s]
+        if kind == 2:
+            return q_got.at[s]
         return recv_sem.at[kind] if kind != 1 else pass_got.at[s]
 
     def outward(kind, src, dst, j, r):
@@ -183,6 +185,14 @@
         return carry
 
     lax.fori_loop(0, 8, send_k, 0)
+
+    def send_seg(t, carry):
+        j = turns(t)
+        for r in range(2):
+            send(part_of(3, j, r), j, r)
+        return carry
+
+    lax.fori_loop(0, 8, send_seg, 0)
     loads[6].wait()
     q_wide[...] = q_raw[...].astype(F32).reshape(TOK * 16, HD)
 
@@ -198,13 +208,6 @@
 
     lax.fori_loop(0, 8, send_q, 0)
 
-    def send_seg(t, carry):
-        j = turns(t)
-        for r in range(2):
-            send(part_of(3, j, r), j, r)
-        return carry
-
-    lax.fori_loop(0, 8, send_seg, 0)
     loads[7].wait()
     v_wide[...] = v_raw[...].astype(F32).reshape(TOK * 8, HD)
 
@@ -256,7 +259,6 @@
     def _():
         lax.fori_loop(0, SEQ, forward, 0)
 
-    wait_on(q_all, recv_sem.at[2])
     wait_on(seg_all, recv_sem.at[3])
 
     @pl.when(core == 1)
@@ -319,13 +321,10 @@
             prob[qi, d] = (expo[d] * inv).astype(BF16)
 
     def forward_step(i, carry):
-        by_queries(turns(i), forward_block)
-
-        @pl.when(core == 1)
-        def _():
-            forward(2 * i, 0)
-            forward(2 * i + 1, 0)
-
+        qi = lax.rem(j_own + NBLK - i, NBLK)
+        for half in range(2):
+            wait_on(q_all.at[2 * qi + half], q_got.at[2 * qi + half])
+        by_queries(qi, forward_block)
         return carry
 
     lax.fori_loop(0, NBLK, forward_step, 0)
@@ -337,6 +336,11 @@
         return carry
 
     lax.fori_loop(0, SEQ, units, 0)
+
+    @pl.when(core == 1)
+    def _():
+        lax.fori_loop(0, SEQ, forward, 0)
+
 
     @pl.when(core == 0)
     def _():
@@ -632,7 +636,7 @@
             pltpu.VMEM(tiles, BF16), pltpu.VMEM(tiles, BF16),
             pltpu.VMEM((2, 8, HD), F32), pltpu.VMEM((2, 32, 8, HD), F32),
             pltpu.VMEM((2, 1, HD), F32),
-            dma((9,)), dma((4,)), dma((4,)), dma, dma, dma((SEQ,)), dma((SEQ,)),
+            dma((9,)), dma((4,)), dma((4,)), dma, dma, dma((SEQ,)), dma((SEQ,)), dma((SEQ,)),
             dma((2,)), dma((2,)), dma, dma((SEQ,)), dma((2,)), dma((2,)), dma((5,)),
         ],
         compiler_params=pltpu.CompilerParams(

time: 61.2 us -> 60.7 us (level)
  no operation moved by 1% of the time
where the time goes in v6:
time: 60.7 us; the launch traced here: 60.6 us
  Pallas kernels  59.9 us (99%)
  between operations  0.64 us (1%)
    pallas_call x1, Pallas kernels, body(): pl.pallas_call(fused_kernel, name='heads_and_back', out_shape=kinds, in_s...  58.9 us

profile of v6, /device:TPU:1, one launch (start us, length us, event | category | flops | bytes accessed | tf_op | source)
XLA Modules:
  0.0 60.6 jit_solution(2501007860619405652)
XLA Ops:
  0.6 58.9 %heads_and_back.1 = (bf16[128,16,128]{2,1,0:T(8,128)(2,1)S(1)}, bf16[128,8,128]{2,1,0:T(8,128)(2,1)S(1)}, bf16[128,8,128]{2,1,0:T(8,128)(2,1)S(1)}, f32[1,128]{1,0:T(1,128)S(1)}, f32[1,128]{1,0:T(1,128)S(1)}) custom-call(bf16[128,16,128]{2,1,0:T(8,128)(2,1)} %bitcast.11, bf16[128,8,128]{2,1,0:T(8,128)(2,1)} %bitcast.13, bf16[128,8,128]{2,1,0:T(8,128)(2,1)} %bitcast.14, ...), custom_call_target="tpu_custom_call" | custom-call | tf_op jit(solution)/shard_map/heads_and_back/pallas_call | solution.py:609
  59.5 1.0 %store_results.1 = (bf16[128,16,128]{2,1,0:T(8,128)(2,1)}, bf16[128,8,128]{2,1,0:T(8,128)(2,1)}, bf16[128,8,128]{2,1,0:T(8,128)(2,1)}, f32[1,128]{1,0:T(1,128)}, f32[1,128]{1,0:T(1,128)}) custom-call(bf16[128,16,128]{2,1,0:T(8,128)(2,1)S(1)} %get-tuple-element.15.q_ref, bf16[128,8,128]{2,1,0:T(8,128)(2,1)S(1)} %get-tuple-element.16.k_ref, ...), custom_call_target="tpu_custom_call" | custom-call | tf_op jit(solution)/shard_map/store_results/pallas_call | solution.py:652
